TPU v7x, 32 devices: a whole 2x2x4 slice. The times are simulated.
32 devices in a mesh: groups: 2 (over y), row: 4 (over z), col: 2 (over x), sub: 2 (over core).
Axes of the slice: x: 2, y: 2, z: 4, core: 2. Of those that a mesh axis runs over, the one named last changes fastest.
Arguments:
- features: bfloat16 [1024, 512, 256], P(('groups', 'row', 'sub'), 'col'), parts along dimension 0, may hold values from -96 to 96
- seeds: int32 [1024, 512], P(('groups', 'row', 'sub'), 'col'), parts along dimension 0, may hold values from 0 to 64, as said below
- valid_tiles: int32 [8, 2], P(('groups', 'row'), 'col'), parts along dimension 0, may hold values from 0 to 1, as said below
- prototypes: bfloat16 [128, 4, 256], P('groups'), parts along dimension 0, may hold values from -1 to 1
Outputs:
- refined_protos: float32 [128, 4, 256], P('groups'), parts along dimension 0
- beliefs: float32 [128, 512, 512], P('groups', ('row', 'sub'), 'col'), parts along dimension 0
There are 2 independent parts, one for each index of `groups`. A program takes and returns all parts, laid end to end along the dimension named above; each array names one. Nothing has to cross between parts.
Inputs may be any that keep to these rules, and one draw needn't show every extreme that they name: seeds[h, w] is a token's seed class, or 64 for a token without a seed. `valid_tiles`: every region has at least one masked and at least one usable tile.
All inputs are finite; a program needn't handle non-finite values.
Results may differ from a plain program's by a relative error of at most 0.0066.
Values sent between devices are 32-bit elements; how exact they have to be, the bound alone decides.
No kernel may reach another device: no remote copies, remote signals or barrier semaphores. Data moves between devices by JAX's collectives and lax.ppermute only.
A program may use at most 128 MiB of HBM per device.

v0:
```python
import functools
import math

import jax
import jax.numpy as jnp
import numpy as np
from jax import lax
from jax.experimental import pallas as pl
from jax.experimental.pallas import tpu as pltpu
from jax.sharding import PartitionSpec as P

ITERS = 2
SCALE = 2.0
SEED_REWARD = 2.0
LOW = -1e30
REACH = 3
HALO = ITERS * REACH
LANES = 128
STATS = 8
PACK = 16
GAIN = 1.461325
TAPS = [math.exp(-(d * d) / 8.0) / GAIN for d in range(REACH + 1)]
F32 = jnp.float32
BF16 = jnp.bfloat16


def cost(flops, moved):
    return pl.CostEstimate(flops=flops, bytes_accessed=moved, transcendentals=0)


def across_taps(cols):
    place = np.full(cols + LANES, -(10**6))
    place[:cols] = np.arange(cols)
    place[cols : cols + HALO] = np.arange(-HALO, 0)
    place[cols + HALO : cols + 2 * HALO] = np.arange(cols, cols + HALO)
    gap = np.abs(place[:, None] - place[None, :])
    used = (place[:, None] > -(10**5)) & (place[None, :] > -(10**5)) & (gap <= REACH)
    return np.where(used, GAIN * np.exp(-np.minimum(gap, REACH) ** 2 / 8.0), 0.0)


def pool_kernel(meta, seeds, feats, protos, keep, give, score, weight, acc, peak, total):
    rows, cols, chans = feats.shape
    count = protos.shape[0]
    classes = count // 4
    step = pl.program_id(0)

    @pl.when(step == 0)
    def _():
        acc[...] = jnp.zeros_like(acc)
        total[...] = jnp.zeros_like(total)
        peak[...] = jnp.full_like(peak, LOW)

    labels = lax.broadcasted_iota(jnp.int32, (classes, cols), 0)
    top = jnp.full((count, LANES), LOW, F32)
    for r in range(rows):
        here = jnp.where(meta[0] > 0, seeds[r : r + 1, :], -1)
        member = here == labels
        raw = lax.dot_general(
            protos[...], feats[r], (((1,), (1,)), ((), ())), preferred_element_type=F32
        )
        masked = jnp.concatenate(
            [
                jnp.where(member, raw[m * classes : (m + 1) * classes], LOW)
                for m in range(count // classes)
            ],
            axis=0,
        )
        score[:, r * cols : (r + 1) * cols] = masked
        for c in range(cols // LANES):
            top = jnp.maximum(top, masked[:, c * LANES : (c + 1) * LANES])
    before = peak[...]
    after = jnp.maximum(before, jnp.max(top, axis=1, keepdims=True))
    fade = jnp.exp(before - after)
    shift = jnp.maximum(after, 0.1 * LOW)
    gained = jnp.zeros((count, LANES), F32)
    for c in range(rows * cols // LANES):
        part = jnp.exp(score[:, c * LANES : (c + 1) * LANES] - shift)
        gained = gained + part
        weight[:, c * LANES : (c + 1) * LANES] = part.astype(BF16)
    peak[...] = after
    total[...] = total[...] * fade + gained
    flat = feats[...].reshape(rows * cols, chans)
    acc[...] = acc[...] * fade[:, :1] + jnp.dot(weight[...], flat, preferred_element_type=F32)

    @pl.when(step == pl.num_programs(0) - 1)
    def _():
        sub = meta[1]
        sums = acc[...].T
        tops = peak[...].T[:1]
        totals = jnp.sum(total[...].T, axis=0, keepdims=True)
        half = count // 2

        def write(ref, second):
            lanes = slice(half, count) if second else slice(0, half)
            ref[:chans, :] = sums[:, lanes]
            ref[chans : chans + 1, :] = tops[:, lanes]
            ref[chans + 1 : chans + 2, :] = totals[:, lanes]
            ref[chans + 2 :, :] = jnp.zeros((STATS - 2, half), F32)

        @pl.when(sub == 0)
        def _():
            write(keep, False)
            write(give, True)

        @pl.when(sub != 0)
        def _():
            write(keep, True)
            write(give, False)


def pool(meta, seeds, feats, protos):
    height, cols, chans = feats.shape
    count = protos.shape[0]
    rows = 8
    piece = jax.ShapeDtypeStruct((chans + STATS, count // 2), F32)
    whole = pl.BlockSpec((chans + STATS, count // 2), lambda i, *_: (0, 0))
    return pl.pallas_call(
        pool_kernel,
        out_shape=(piece, piece),
        grid_spec=pltpu.PrefetchScalarGridSpec(
            num_scalar_prefetch=1,
            grid=(height // rows,),
            in_specs=[
                pl.BlockSpec((rows, cols), lambda i, *_: (i, 0)),
                pl.BlockSpec((rows, cols, chans), lambda i, *_: (i, 0, 0)),
                pl.BlockSpec((count, chans), lambda i, *_: (0, 0)),
            ],
            out_specs=(whole, whole),
            scratch_shapes=[
                pltpu.VMEM((count, rows * cols), F32),
                pltpu.VMEM((count, rows * cols), BF16),
                pltpu.VMEM((count, chans), F32),
                pltpu.VMEM((count, LANES), F32),
                pltpu.VMEM((count, LANES), F32),
            ],
        ),
        compiler_params=pltpu.CompilerParams(vmem_limit_bytes=24 << 20),
        cost_estimate=cost(4 * height * cols * chans * count, height * cols * chans * 2),
        name="pool",
    )(meta, seeds, feats, protos)


def merge_kernel(a, b, out):
    chans = a.shape[0] - STATS
    at, bt = a[chans : chans + 1, :], b[chans : chans + 1, :]
    top = jnp.maximum(at, bt)
    fa, fb = jnp.exp(at - top), jnp.exp(bt - top)
    out[:chans, :] = a[:chans, :] * fa + b[:chans, :] * fb
    out[chans : chans + 1, :] = top
    out[chans + 1 : chans + 2, :] = (
        a[chans + 1 : chans + 2, :] * fa + b[chans + 1 : chans + 2, :] * fb
    )
    out[chans + 2 :, :] = jnp.zeros((STATS - 2, a.shape[1]), F32)


def merge(a, b):
    return pl.pallas_call(
        merge_kernel,
        out_shape=jax.ShapeDtypeStruct(a.shape, F32),
        in_specs=[pl.BlockSpec(memory_space=pltpu.VMEM)] * 2,
        out_specs=pl.BlockSpec(memory_space=pltpu.VMEM),
        cost_estimate=cost(3 * a.size, 12 * a.size),
        name="merge",
    )(a, b)


def field_kernel(
    meta, keep, got, near, far, codes, strip, strip_codes, taps, feats,
    refined, out,
    held, base, belief, second, lhs, sums, mixed, result, sem, out_sem,
):
    height, cols, chans = feats.shape
    count = sums.shape[1]
    classes = count // 4
    wide = cols + LANES
    sub = meta[1]
    groups = 8

    def fetch(i):
        rows = height // groups
        return pltpu.make_async_copy(
            feats.at[pl.ds(i * rows, rows)], held.at[pl.ds(i * rows, rows)], sem.at[i]
        )

    for i in range(groups):
        fetch(i).start()

    half = count // 2
    first = pl.multiple_of(sub * half, half)
    other = pl.multiple_of((1 - sub) * half, half)
    sums[:, pl.ds(first, half)] = keep[...]
    sums[:, pl.ds(other, half)] = got[...]
    pooled = sums[:chans, :] / sums[chans + 1 : chans + 2, :]
    length = jnp.sqrt(jnp.sum(pooled * pooled, axis=0, keepdims=True) + 1e-06)
    ready = (pooled / length).T
    for c in range(chans // LANES):
        lanes = slice(c * LANES, (c + 1) * LANES)
        for m in range(4):
            mixed[c, pl.ds(m, classes, stride=4), :] = ready[m * classes : (m + 1) * classes, lanes]
        refined[:, lanes] = mixed[c]
    lead = (ready.astype(BF16).astype(F32) * SCALE).astype(BF16)

    labels = lax.broadcasted_iota(jnp.int32, (classes, 1), 0) + 1
    bonus = math.exp(SEED_REWARD)

    def unary(tokens, code):
        raw = lax.dot_general(lead, tokens, (((1,), (1,)), ((), ())), preferred_element_type=F32)
        parts = [raw[m * classes : (m + 1) * classes] for m in range(4)]
        top = functools.reduce(jnp.maximum, parts)
        top = jnp.max(top, axis=0, keepdims=True)
        top = jnp.where(code == 0, 1e30, top)
        grown = functools.reduce(jnp.add, [jnp.exp(part - top) for part in parts])
        grown = jnp.where(labels == code, grown * bonus, grown)
        return grown, share(grown)

    def share(grown):
        norm = jnp.sum(grown, axis=0, keepdims=True)
        return grown * (1.0 / jnp.maximum(norm, 1e-30))

    def edge(ref, i, row):
        tokens = ref[pl.ds(pl.multiple_of(i * cols, cols), cols), :].astype(BF16)
        code = ref[pl.ds(HALO * cols + i, 1), :].astype(jnp.int32)
        grown, first_belief = unary(tokens, code)
        base[row, :, :cols] = grown
        belief[row, :, :cols] = first_belief

    near_at = jnp.where(sub == 0, HALO + height, 0)
    far_at = jnp.where(sub == 0, 0, HALO + height)

    @pl.loop(0, HALO)
    def _(i):
        edge(near, i, near_at + i)
        edge(far, i, far_at + i)

    for g in range(strip.shape[0]):
        grown, first_belief = unary(strip[g], strip_codes[g : g + 1, :])
        for r in range(LANES // PACK):
            row = g * (LANES // PACK) + r
            if row < height + 2 * HALO:
                turn = (LANES - r * PACK) % LANES
                base[row, :, cols:] = pltpu.roll(grown, turn, 1) if turn else grown
                belief[row, :, cols:] = pltpu.roll(first_belief, turn, 1) if turn else first_belief

    for i in range(groups):
        fetch(i).wait()
        rows = height // groups

        @pl.loop(0, rows)
        def _(j):
            row = i * rows + j
            grown, first_belief = unary(held[row], codes[pl.ds(row, 1), :])
            base[HALO + row, :, :cols] = grown
            belief[HALO + row, :, :cols] = first_belief

    def mix(source, row, slot):
        centre = source[row]
        tall = TAPS[0] * centre
        for d in range(1, REACH + 1):
            tall = tall + TAPS[d] * (source[row - d] + source[row + d])
        high = tall.astype(BF16)
        low = (tall - high.astype(F32)).astype(BF16)
        at = pl.ds(slot * classes, classes)
        lhs[at, :cols] = high[:, :cols]
        lhs[at, cols : 2 * cols] = low[:, :cols]
        lhs[at, 2 * cols : 2 * cols + LANES] = high[:, cols:]
        lhs[at, 2 * cols + LANES :] = low[:, cols:]

    batch = 7

    @pl.loop(0, (height + 2 * REACH) // batch)
    def _(i):
        start = REACH + i * batch
        for j in range(batch):
            mix(belief, start + j, j)
        message = jnp.dot(lhs[: batch * classes, :], taps[...], preferred_element_type=F32)
        for j in range(batch):
            row = start + j
            sent = message[j * classes : (j + 1) * classes, :] - belief[row]
            second[row] = share(base[row] * jnp.exp(sent))

    batch = 8
    tiles = cols // LANES
    flat = result.reshape(tiles * classes * height, LANES)

    def leave(i, c):
        rows = pl.ds(pl.multiple_of(i * batch, batch), batch)
        return pltpu.make_async_copy(
            result.at[c, :, rows, :],
            out.at[:, rows, pl.ds(c * LANES, LANES)],
            out_sem.at[i, c],
        )

    @pl.loop(0, height // batch)
    def _(i):
        start = HALO + i * batch
        for j in range(batch):
            mix(second, start + j, j)
        message = jnp.dot(
            lhs[: batch * classes, :], taps[:, :cols], preferred_element_type=F32
        )
        for j in range(batch):
            row = start + j
            sent = message[j * classes : (j + 1) * classes, :] - second[row, :, :cols]
            done = share(base[row, :, :cols] * jnp.exp(sent))
            for c in range(tiles):
                at = c * classes * height + row - HALO
                flat[pl.ds(at, classes, stride=height), :] = done[:, c * LANES : (c + 1) * LANES]
        for c in range(tiles):
            leave(i, c).start()

    @pl.loop(0, height // batch)
    def _(i):
        for c in range(tiles):
            leave(i, c).wait()


def field(meta, keep, got, near, far, codes, strip, strip_codes, feats, count):
    height, cols, chans = feats.shape
    classes = count // 4
    wide = cols + LANES
    deep = height + 2 * HALO
    across = across_taps(cols)
    taps = np.concatenate([across[:cols], across[:cols], across[cols:], across[cols:]], axis=0)
    vmem = pl.BlockSpec(memory_space=pltpu.VMEM)
    return pl.pallas_call(
        field_kernel,
        out_shape=(
            jax.ShapeDtypeStruct((count, chans), F32),
            jax.ShapeDtypeStruct((classes, height, cols), F32),
        ),
        in_specs=[pl.BlockSpec(memory_space=pltpu.SMEM)]
        + [vmem] * 8
        + [pl.BlockSpec(memory_space=pl.ANY)],
        out_specs=(vmem, pl.BlockSpec(memory_space=pl.ANY)),
        scratch_shapes=[
            pltpu.VMEM((height, cols, chans), BF16),
            pltpu.VMEM((deep, classes, wide), F32),
            pltpu.VMEM((deep, classes, wide), F32),
            pltpu.VMEM((deep, classes, wide), F32),
            pltpu.VMEM((8 * classes, 2 * wide), BF16),
            pltpu.VMEM((chans + STATS, count), F32),
            pltpu.VMEM((chans // LANES, count, LANES), F32),
            pltpu.VMEM((cols // LANES, classes, height, LANES), F32),
            pltpu.SemaphoreType.DMA((8,)),
            pltpu.SemaphoreType.DMA((height // 8, cols // LANES)),
        ],
        compiler_params=pltpu.CompilerParams(vmem_limit_bytes=56 << 20),
        cost_estimate=cost(8 * height * cols * chans * count, 16 << 20),
        name="field",
    )(meta, keep, got, near, far, codes, strip, strip_codes, jnp.asarray(taps, BF16), feats)


def swap(x, axes, pairs):
    return lax.ppermute(x, axes, [p for a, b in pairs for p in ((a, b), (b, a))])


def on_device(features, seeds, valid_tiles, prototypes):
    height, cols, chans = features.shape
    classes, modes, _ = prototypes.shape
    count = classes * modes
    n_row, n_col = lax.axis_size("row"), lax.axis_size("col")
    sub, col = lax.axis_index("sub"), lax.axis_index("col")
    meta = jnp.stack([valid_tiles[0, 0], sub]).astype(jnp.int32)
    codes = jnp.where(valid_tiles[0, 0] > 0, seeds + 1, 0)
    protos = (SCALE * prototypes.astype(F32)).astype(BF16)
    protos = protos.transpose(1, 0, 2).reshape(count, chans)

    def edge_rows(start):
        rows = lax.dynamic_slice_in_dim(features, start, HALO, axis=0).astype(F32)
        marks = lax.dynamic_slice_in_dim(codes, start, HALO, axis=0).astype(F32)
        return jnp.concatenate([rows.reshape(-1, chans), marks.reshape(-1, chans)], axis=0)

    low_edge = height - HALO
    near = swap(edge_rows(jnp.where(sub == 0, low_edge, 0)), "sub", [(0, 1)])
    far = swap(
        edge_rows(jnp.where(sub == 0, 0, low_edge)),
        ("row", "sub"),
        [(2 * i + 1, 2 * i + 2) for i in range(n_row - 1)],
    )

    keep, give = pool(meta, seeds, features, protos)
    keep = merge(keep, swap(give, "sub", [(0, 1)]))
    stride = 1
    while stride < n_col:
        pairs = [(i, i | stride) for i in range(n_col) if not i & stride]
        keep = merge(keep, swap(keep, "col", pairs))
        stride *= 2
    stride = 1
    while stride < n_row:
        pairs = [(i, i | stride) for i in range(n_row) if not i & stride]
        keep = merge(keep, swap(keep, "row", pairs))
        stride *= 2
        if stride == 2:
            keep, near, far = lax.optimization_barrier((keep, near, far))

            def edge_cols(start):
                def cut(msg):
                    rows = msg[: HALO * cols].reshape(HALO, cols, chans)
                    marks = msg[HALO * cols :].reshape(HALO, cols)
                    return (
                        lax.dynamic_slice_in_dim(rows, start, HALO, axis=1),
                        lax.dynamic_slice_in_dim(marks, start, HALO, axis=1),
                    )

                near_part, far_part = cut(near), cut(far)
                mine = (
                    lax.dynamic_slice_in_dim(features, start, HALO, axis=1).astype(F32),
                    lax.dynamic_slice_in_dim(codes, start, HALO, axis=1).astype(F32),
                )
                rows, marks = (
                    jnp.concatenate(
                        [
                            jnp.where(sub == 0, f, n),
                            o,
                            jnp.where(sub == 0, n, f),
                        ],
                        axis=0,
                    )
                    for n, o, f in zip(near_part, mine, far_part)
                )
                rows = rows.reshape(-1, chans)
                marks = marks.reshape(-1)
                marks = jnp.pad(marks, (0, -marks.shape[0] % chans)).reshape(-1, chans)
                return jnp.concatenate([rows, marks], axis=0)

            even = col % 2 == 0
            right_edge = cols - HALO
            one = swap(
                edge_cols(jnp.where(even, right_edge, 0)),
                "col",
                [(i, i + 1) for i in range(0, n_col - 1, 2)],
            )
            if n_col > 2:
                two = swap(
                    edge_cols(jnp.where(even, 0, right_edge)),
                    "col",
                    [(i, i + 1) for i in range(1, n_col - 1, 2)],
                )
            else:
                two = jnp.zeros_like(one)
    got = swap(keep, "sub", [(0, 1)])

    deep = height + 2 * HALO
    left = jnp.where(even, two, one)
    right = jnp.where(even, one, two)

    def unpack(msg):
        rows = msg[: deep * HALO].reshape(deep, HALO, chans)
        marks = msg[deep * HALO :].reshape(-1)[: deep * HALO].reshape(deep, HALO)
        return rows, marks

    (left_rows, left_marks), (right_rows, right_marks) = unpack(left), unpack(right)
    per = LANES // PACK
    more = (-deep % per, PACK - 2 * HALO)
    strip = jnp.concatenate([left_rows, right_rows], axis=1).astype(BF16)
    strip = jnp.pad(strip, ((0, more[0]), (0, more[1]), (0, 0))).reshape(-1, LANES, chans)
    marks = jnp.concatenate([left_marks, right_marks], axis=1).astype(jnp.int32)
    marks = jnp.pad(marks, ((0, more[0]), (0, more[1]))).reshape(-1, LANES)

    refined, belief = field(meta, keep, got, near, far, codes, strip, marks, features, count)
    return refined.reshape(classes, modes, chans), belief


def solution(mesh):
    placed = (
        P(("groups", "row", "sub"), "col", None),
        P(("groups", "row", "sub"), "col"),
        P(("groups", "row"), "col"),
        P("groups", None, None),
    )
    return jax.shard_map(
        on_device,
        mesh=mesh,
        in_specs=placed,
        out_specs=(P("groups", None, None), P("groups", ("row", "sub"), "col")),
        check_vma=False,
    )
```

profile of v0, /device:TPU:0, one launch (start us, length us, event | category | flops | bytes accessed | tf_op | source)
XLA Modules:
  0.0 112.9 jit_solution(653011536578384335)
XLA Ops:
  2.2 1.5 %constant_dynamic-slice_fusion = (bf16[6,256,256]{2,1,0:T(8,128)(2,1)S(1)}, bf16[6,256,256]{2,1,0:T(8,128)(2,1)S(1)}) fusion(bf16[64,256,256]{2,1,0:T(8,128)(2,1)} %feats.3, s32[]{:T(128)S(6)} %select_n.74, s32[]{:T(128)S(6)} %select_n.71), kind=kLoop, calls=%fused_computation.31 | loop fusion | bytes 3145736 | tf_op jit(solution)/shard_map/dynamic_slice | solution.py:369
  3.8 1.2 %pad_maximum_fusion = f32[1542,256]{1,0:T(8,128)} fusion(f32[6,256]{1,0:T(8,128)S(1)} %get-tuple-element.23, f32[1536,256]{1,0:T(8,128)S(1)} %bitcast_convert_fusion.1), kind=kLoop, calls=%fused_computation | loop fusion | flops 394752 | bytes 3158016 | tf_op jit(solution)/shard_map/concatenate | solution.py:371
  5.7 1.3 %pad_maximum_fusion.1 = f32[1542,256]{1,0:T(8,128)} fusion(f32[6,256]{1,0:T(8,128)S(1)} %get-tuple-element.22, f32[1536,256]{1,0:T(8,128)S(1)} %bitcast_convert_fusion), kind=kLoop, calls=%fused_computation.1 | loop fusion | flops 394752 | bytes 3158016 | tf_op jit(solution)/shard_map/concatenate | solution.py:371
  7.0 2.0 %collective-permute-start.4 = (f32[1542,256]{1,0:T(8,128)}, f32[1542,256]{1,0:T(8,128)}, u32[]{:S(2)}, u32[]{:S(2)}) collective-permute-start(f32[1542,256]{1,0:T(8,128)} %pad_maximum_fusion.1), channel_id=1, source_target_pairs={{1,4},{4,1},{5,8},{8,5},{9,12},{12,9},{3,6},{6,3},{7,10},{10,7},{1... | collective-permute-start | bytes 4737032 | tf_op jit(solution)/shard_map/ppermute | solution.py:354
  9.2 15.6 %pool.1 = (f32[264,128]{1,0:T(8,128)S(1)}, f32[264,128]{1,0:T(8,128)S(1)}) custom-call(s32[2]{0:T(128)S(1)} %pad_add_fusion.meta, s32[64,256]{1,0:T(8,128)S(1)} %copy-done.2, bf16[64,256,256]{2,1,0:T(8,128)(2,1)S(1)} %copy-done, bf16[256,256]{1,0:T(8,128)(2,1)S(1)} %bitcast.24), custom_call_target="tpu_custom_call" | custom-call | flops 4294967296 | bytes 8388608 | tf_op jit(solution)/shard_map/pool/pallas_call | solution.py:117
  25.5 2.9 %collective-permute-start = (f32[264,128]{1,0:T(8,128)S(1)}, f32[264,128]{1,0:T(8,128)S(1)}, u32[]{:S(2)}, u32[]{:S(2)}) collective-permute-start(f32[264,128]{1,0:T(8,128)S(1)} %get-tuple-element.10), channel_id=1, source_target_pairs={{0,1},{1,0},{2,3},{3,2},{4,5},{5,4},{6,7},{7,6},{8,9},{9,8},{10,11... | collective-permute-start | bytes 405512 | tf_op jit(solution)/shard_map/ppermute | solution.py:354
  28.4 1.0 collective-permute-done.b
  30.0 1.7 %merge.4.a = f32[264,128]{1,0:T(8,128)} custom-call(f32[264,128]{1,0:T(8,128)} %copy-done.1, f32[264,128]{1,0:T(8,128)} %copy-done.8), custom_call_target="tpu_custom_call" | custom-call | flops 101376 | bytes 405504 | tf_op jit(solution)/shard_map/merge/pallas_call | solution.py:157
  31.7 1.5 %collective-permute-start.1 = (f32[264,128]{1,0:T(8,128)}, f32[264,128]{1,0:T(8,128)S(1)}, u32[]{:S(2)}, u32[]{:S(2)}) collective-permute-start(f32[264,128]{1,0:T(8,128)} %merge.4.a), channel_id=1, source_target_pairs={{0,2},{2,0},{1,3},{3,1},{4,6},{6,4},{5,7},{7,5},{8,10},{10,8},{9,1... | collective-permute-start | bytes 405512 | tf_op jit(solution)/shard_map/ppermute | solution.py:354
  33.2 4.6 %collective-permute-done.1.b = f32[264,128]{1,0:T(8,128)S(1)} collective-permute-done((f32[264,128]{1,0:T(8,128)}, f32[264,128]{1,0:T(8,128)S(1)}, u32[]{:S(2)}, u32[]{:S(2)}) %collective-permute-start.1) | collective-permute-done | bytes 135200 | tf_op jit(solution)/shard_map/ppermute | solution.py:354
  38.4 1.6 %merge.5.a = f32[264,128]{1,0:T(8,128)} custom-call(f32[264,128]{1,0:T(8,128)} %merge.4.a, f32[264,128]{1,0:T(8,128)} %copy-done.7), custom_call_target="tpu_custom_call" | custom-call | flops 101376 | bytes 405504 | tf_op jit(solution)/shard_map/merge/pallas_call | solution.py:157
  40.0 1.6 %collective-permute-start.2 = (f32[264,128]{1,0:T(8,128)}, f32[264,128]{1,0:T(8,128)S(1)}, u32[]{:S(2)}, u32[]{:S(2)}) collective-permute-start(f32[264,128]{1,0:T(8,128)} %merge.5.a), channel_id=1, source_target_pairs={{0,4},{4,0},{8,12},{12,8},{1,5},{5,1},{9,13},{13,9},{2,6},{6,2},{1... | collective-permute-start | bytes 405512 | tf_op jit(solution)/shard_map/ppermute | solution.py:354
  41.7 1.0 dynamic-slice_convert_fusion
  42.7 2.6 %collective-permute-done.2.b = f32[264,128]{1,0:T(8,128)S(1)} collective-permute-done((f32[264,128]{1,0:T(8,128)}, f32[264,128]{1,0:T(8,128)S(1)}, u32[]{:S(2)}, u32[]{:S(2)}) %collective-permute-start.2) | collective-permute-done | bytes 135200 | tf_op jit(solution)/shard_map/ppermute | solution.py:354
  45.9 1.6 %merge.6.a = f32[264,128]{1,0:T(8,128)} custom-call(f32[264,128]{1,0:T(8,128)} %merge.5.a, f32[264,128]{1,0:T(8,128)} %copy-done.9), custom_call_target="tpu_custom_call" | custom-call | flops 101376 | bytes 405504 | tf_op jit(solution)/shard_map/merge/pallas_call | solution.py:157
  47.6 1.1 %copy-done.4 = f32[1542,256]{1,0:T(8,128)} copy-done((f32[1542,256]{1,0:T(8,128)}, f32[1542,256]{1,0:T(8,128)S(1)}, u32[]{:S(2)}) %copy-start.4) | copy-done | bytes 1579032
  49.4 2.8 %slice.32 = f32[1536,256]{1,0:T(8,128)} slice(f32[1542,256]{1,0:T(8,128)} %collective-permute-done.4.far), slice={[0:1536], [0:256]} | slice | bytes 3145728 | tf_op jit(solution)/shard_map/slice | solution.py:398
  53.5 1.6 %collective-permute-start.7 = (f32[458,256]{1,0:T(8,128)S(1)}, f32[458,256]{1,0:T(8,128)S(1)}, u32[]{:S(2)}, u32[]{:S(2)}) collective-permute-start(f32[458,256]{1,0:T(8,128)S(1)} %pad_maximum_fusion.3), channel_id=1, source_target_pairs={{0,2},{2,0},{1,3},{3,1},{4,6},{6,4},{5,7},{7,5},{8,10},{10,8},{9,1... | collective-permute-start | bytes 1406984 | tf_op jit(solution)/shard_map/ppermute | solution.py:354
  55.0 2.6 %collective-permute-start.5 = (f32[264,128]{1,0:T(8,128)S(1)}, f32[264,128]{1,0:T(8,128)S(1)}, u32[]{:S(2)}, u32[]{:S(2)}) collective-permute-start(f32[264,128]{1,0:T(8,128)S(1)} %copy-done.5), channel_id=1, source_target_pairs={{0,8},{8,0},{4,12},{12,4},{1,9},{9,1},{5,13},{13,5},{2,10},{10,2},... | collective-permute-start | bytes 405512 | tf_op jit(solution)/shard_map/ppermute | solution.py:354
  57.6 4.8 %collective-permute-done.5.b = f32[264,128]{1,0:T(8,128)S(1)} collective-permute-done((f32[264,128]{1,0:T(8,128)S(1)}, f32[264,128]{1,0:T(8,128)S(1)}, u32[]{:S(2)}, u32[]{:S(2)}) %collective-permute-start.5) | collective-permute-done | bytes 135200 | tf_op jit(solution)/shard_map/ppermute | solution.py:354
  63.1 1.7 %merge.7.keep = f32[264,128]{1,0:T(8,128)} custom-call(f32[264,128]{1,0:T(8,128)} %merge.6.a, f32[264,128]{1,0:T(8,128)} %copy-done.10), custom_call_target="tpu_custom_call" | custom-call | flops 101376 | bytes 405504 | tf_op jit(solution)/shard_map/merge/pallas_call | solution.py:157
  66.3 1.1 fusion.5
  68.1 43.1 %field.1 = (f32[256,256]{1,0:T(8,128)}, f32[64,64,256]{2,1,0:T(8,128)}) custom-call(s32[2]{0:T(128)} %copy-done.3, f32[264,128]{1,0:T(8,128)} %merge.7.keep, f32[264,128]{1,0:T(8,128)} %copy-done.12, f32[1542,256]{1,0:T(8,128)} %copy-done.4, f32[1542,256]{1,0:T(8,128)} %collective-permute-done.4.far, s32[64,256]{1,0:T(8,128)} %copy-done.6, ...), custom_call_target="tpu_custom_call" | custom-call | flops 8589934592 | bytes 16777216 | tf_op jit(solution)/shard_map/field/pallas_call | solution.py:325
  111.2 1.7 %reshape.83 = f32[64,4,256]{2,1,0:T(4,128)} reshape(f32[256,256]{1,0:T(8,128)} %get-tuple-element.14) | data formatting | bytes 524288 | tf_op jit(solution)/shard_map/reshape | solution.py:461
  (69 shorter events, 9.3 us)
Async XLA Ops:
  2.1 39.5 %copy-start.6 = (s32[64,256]{1,0:T(8,128)}, s32[64,256]{1,0:T(8,128)S(1)}, u32[]{:S(2)}) copy-start(s32[64,256]{1,0:T(8,128)S(1)} %add_select_fusion.codes) | copy-start | bytes 196612
  3.8 5.3 %copy-start = (bf16[64,256,256]{2,1,0:T(8,128)(2,1)S(1)}, bf16[64,256,256]{2,1,0:T(8,128)(2,1)}, u32[]{:S(2)}) copy-start(bf16[64,256,256]{2,1,0:T(8,128)(2,1)} %feats.3) | copy-start | bytes 25165828
  5.1 42.5 %collective-permute-start.3 = (f32[1542,256]{1,0:T(8,128)}, f32[1542,256]{1,0:T(8,128)S(1)}, u32[]{:S(2)}, u32[]{:S(2)}) collective-permute-start(f32[1542,256]{1,0:T(8,128)} %pad_maximum_fusion), channel_id=1, source_target_pairs={{0,1},{1,0},{2,3},{3,2},{4,5},{5,4},{6,7},{7,6},{8,9},{9,8},{10,11... | collective-permute-start | bytes 4737032 | tf_op jit(solution)/shard_map/ppermute | solution.py:354
  5.7 3.3 %copy-start.11 = (bf16[64,4,256]{2,1,0:T(4,128)(2,1)S(1)}, bf16[64,4,256]{2,1,0:T(4,128)(2,1)}, u32[]{:S(2)}) copy-start(bf16[64,4,256]{2,1,0:T(4,128)(2,1)} %param.8) | copy-start | bytes 393220
  5.7 3.4 %copy-start.2 = (s32[64,256]{1,0:T(8,128)S(1)}, s32[64,256]{1,0:T(8,128)}, u32[]{:S(2)}) copy-start(s32[64,256]{1,0:T(8,128)} %seeds.1) | copy-start | bytes 196612
  7.0 40.6 %collective-permute-start.4 = (f32[1542,256]{1,0:T(8,128)}, f32[1542,256]{1,0:T(8,128)}, u32[]{:S(2)}, u32[]{:S(2)}) collective-permute-start(f32[1542,256]{1,0:T(8,128)} %pad_maximum_fusion.1), channel_id=1, source_target_pairs={{1,4},{4,1},{5,8},{8,5},{9,12},{12,9},{3,6},{6,3},{7,10},{10,7},{1... | collective-permute-start | bytes 4737032 | tf_op jit(solution)/shard_map/ppermute | solution.py:354
  9.2 15.6 %copy-start.3 = (s32[2]{0:T(128)}, s32[2]{0:T(128)S(1)}, u32[]{:S(2)}) copy-start(s32[2]{0:T(128)S(1)} %pad_add_fusion.meta) | copy-start | bytes 28
  24.8 0.7 copy-start.1
  25.5 3.9 %collective-permute-start = (f32[264,128]{1,0:T(8,128)S(1)}, f32[264,128]{1,0:T(8,128)S(1)}, u32[]{:S(2)}, u32[]{:S(2)}) collective-permute-start(f32[264,128]{1,0:T(8,128)S(1)} %get-tuple-element.10), channel_id=1, source_target_pairs={{0,1},{1,0},{2,3},{3,2},{4,5},{5,4},{6,7},{7,6},{8,9},{9,8},{10,11... | collective-permute-start | bytes 405512 | tf_op jit(solution)/shard_map/ppermute | solution.py:354
  29.3 0.7 copy-start.8
  31.7 6.1 %collective-permute-start.1 = (f32[264,128]{1,0:T(8,128)}, f32[264,128]{1,0:T(8,128)S(1)}, u32[]{:S(2)}, u32[]{:S(2)}) collective-permute-start(f32[264,128]{1,0:T(8,128)} %merge.4.a), channel_id=1, source_target_pairs={{0,2},{2,0},{1,3},{3,1},{4,6},{6,4},{5,7},{7,5},{8,10},{10,8},{9,1... | collective-permute-start | bytes 405512 | tf_op jit(solution)/shard_map/ppermute | solution.py:354
  37.7 0.7 copy-start.7
  40.0 5.2 %collective-permute-start.2 = (f32[264,128]{1,0:T(8,128)}, f32[264,128]{1,0:T(8,128)S(1)}, u32[]{:S(2)}, u32[]{:S(2)}) collective-permute-start(f32[264,128]{1,0:T(8,128)} %merge.5.a), channel_id=1, source_target_pairs={{0,4},{4,0},{8,12},{12,8},{1,5},{5,1},{9,13},{13,9},{2,6},{6,2},{1... | collective-permute-start | bytes 405512 | tf_op jit(solution)/shard_map/ppermute | solution.py:354
  45.3 0.7 copy-start.9
  47.6 1.2 %copy-start.4 = (f32[1542,256]{1,0:T(8,128)}, f32[1542,256]{1,0:T(8,128)S(1)}, u32[]{:S(2)}) copy-start(f32[1542,256]{1,0:T(8,128)S(1)} %collective-permute-done.3.near) | copy-start | bytes 4737028
  49.4 2.8 %slice-start = ((f32[1542,256]{1,0:T(8,128)}), f32[6,256]{1,0:T(8,128)S(1)}, s32[]{:S(2)}) async-start(f32[1542,256]{1,0:T(8,128)} %copy-done.4), calls=%async_computation | async-start | bytes 16384 | tf_op jit(solution)/shard_map/slice | solution.py:399
  49.4 3.0 %slice-start.1 = ((f32[1542,256]{1,0:T(8,128)}), f32[1536,256]{1,0:T(8,128)S(1)}, s32[]{:S(2)}) async-start(f32[1542,256]{1,0:T(8,128)} %copy-done.4), calls=%async_computation.1 | async-start | bytes 3145728 | tf_op jit(solution)/shard_map/slice | solution.py:398
  53.3 1.8 %copy-start.5 = (f32[264,128]{1,0:T(8,128)S(1)}, f32[264,128]{1,0:T(8,128)}, u32[]{:S(2)}) copy-start(f32[264,128]{1,0:T(8,128)} %merge.6.a) | copy-start | bytes 405508
  53.5 11.3 %collective-permute-start.7 = (f32[458,256]{1,0:T(8,128)S(1)}, f32[458,256]{1,0:T(8,128)S(1)}, u32[]{:S(2)}, u32[]{:S(2)}) collective-permute-start(f32[458,256]{1,0:T(8,128)S(1)} %pad_maximum_fusion.3), channel_id=1, source_target_pairs={{0,2},{2,0},{1,3},{3,1},{4,6},{6,4},{5,7},{7,5},{8,10},{10,8},{9,1... | collective-permute-start | bytes 1406984 | tf_op jit(solution)/shard_map/ppermute | solution.py:354
  55.0 7.4 %collective-permute-start.5 = (f32[264,128]{1,0:T(8,128)S(1)}, f32[264,128]{1,0:T(8,128)S(1)}, u32[]{:S(2)}, u32[]{:S(2)}) collective-permute-start(f32[264,128]{1,0:T(8,128)S(1)} %copy-done.5), channel_id=1, source_target_pairs={{0,8},{8,0},{4,12},{12,4},{1,9},{9,1},{5,13},{13,5},{2,10},{10,2},... | collective-permute-start | bytes 405512 | tf_op jit(solution)/shard_map/ppermute | solution.py:354
  62.4 0.7 copy-start.10
  64.7 2.7 %collective-permute-start.6 = (f32[264,128]{1,0:T(8,128)}, f32[264,128]{1,0:T(8,128)S(1)}, u32[]{:S(2)}, u32[]{:S(2)}) collective-permute-start(f32[264,128]{1,0:T(8,128)} %merge.7.keep), channel_id=1, source_target_pairs={{0,1},{1,0},{2,3},{3,2},{4,5},{5,4},{6,7},{7,6},{8,9},{9,8},{10,11... | collective-permute-start | bytes 405512 | tf_op jit(solution)/shard_map/ppermute | solution.py:354
  67.4 0.7 copy-start.12
where the time goes:
time: 113 us
  Pallas kernels  65.3 us (58%)
  local copies, waits for them, and re-layouts  13.5 us (12%)
  waiting for transfers between devices  12.9 us (11%)
  starting transfers between devices  12.6 us (11%)
  other arithmetic  7.1 us (6%)
  between operations  1.54 us (1%)
    pallas_call x1, Pallas kernels, field(): pl.pallas_call(field_kernel, out_shape=(jax.ShapeDtypeStruct((count, chan...  43.1 us
    pallas_call x1, Pallas kernels, pool(): pl.pallas_call(pool_kernel, out_shape=(piece, piece), grid_spec=pltpu.Pre...  15.6 us
    ppermute x8, waiting for transfers between devices, swap(): lax.ppermute(x, axes, [p for a, b in pairs for p in ((a, b), (b, a))])  12.9 us
    ppermute x8, starting transfers between devices, swap(): lax.ppermute(x, axes, [p for a, b in pairs for p in ((a, b), (b, a))])  12.6 us
    pallas_call x4, Pallas kernels, merge(): pl.pallas_call(merge_kernel, out_shape=jax.ShapeDtypeStruct(a.shape, F32)...  6.59 us
    unnamed x30, local copies, waits for them, and re-layouts  5.23 us
    slice x3, local copies, waits for them, and re-layouts, cut(): rows = msg[:HALO * cols].reshape(HALO, cols, chans)  2.77 us
    concatenate x2, other arithmetic, edge_rows(): jnp.concatenate([rows.reshape(-1, chans), marks.reshape(-1, chans)], axis=0)  2.51 us
  transfers between devices with their start and end apart: 8, of which 4 were waited for; matrix products, arithmetic and copies ran while one was open for 5% of the time, Pallas kernels for 20%

commit v1 on v0

v1 whole, which is shorter than its diff:
```python
import functools
import math

import jax
import jax.numpy as jnp
import numpy as np
from jax import lax
from jax.experimental import pallas as pl
from jax.experimental.pallas import tpu as pltpu
from jax.sharding import PartitionSpec as P

ITERS = 2
SCALE = 2.0
SEED_REWARD = 2.0
LOW = -1e30
REACH = 3
HALO = ITERS * REACH
LANES = 128
STATS = 8
SIDE = 8
GAIN = 1.461325
TAPS = [math.exp(-(d * d) / 8.0) / GAIN for d in range(REACH + 1)]
F32 = jnp.float32
BF16 = jnp.bfloat16
VMEM = pl.BlockSpec(memory_space=pltpu.VMEM)
SMEM = pl.BlockSpec(memory_space=pltpu.SMEM)
ANY = pl.BlockSpec(memory_space=pl.ANY)


def cost(flops, moved):
    return pl.CostEstimate(flops=flops, bytes_accessed=moved, transcendentals=0)


def params(mib):
    return pltpu.CompilerParams(vmem_limit_bytes=mib << 20)


def across_taps(cols, sides):
    both = []
    for odd in (False, True):
        place = np.full(cols + LANES, -(10**6))
        place[:cols] = np.arange(cols)
        right, left = (cols + SIDE, cols) if odd else (cols, cols + SIDE)
        if sides == 2 or not odd:
            place[right : right + HALO] = cols + np.arange(HALO)
        if sides == 2 or odd:
            place[left + SIDE - HALO : left + SIDE] = np.arange(-HALO, 0)
        gap = np.abs(place[:, None] - place[None, :])
        used = (place[:, None] > -(10**5)) & (place[None, :] > -(10**5)) & (gap <= REACH)
        taps = np.where(used, GAIN * np.exp(-np.minimum(gap, REACH) ** 2 / 8.0), 0.0)
        both.append(np.concatenate([taps[:cols], taps[:cols], taps[cols:], taps[cols:]], axis=0))
    return np.stack(both)


def ends_kernel(meta, seeds, feats, near, far, held, sem):
    height, cols, chans = feats.shape
    fetch = [
        pltpu.make_async_copy(feats.at[pl.ds(at, HALO)], held.at[i], sem.at[i])
        for i, at in enumerate((0, height - HALO))
    ]
    for copy in fetch:
        copy.start()
    for copy in fetch:
        copy.wait()

    def write(ref, i):
        at = (0, height - HALO)[i]
        for r in range(HALO):
            ref[r * cols : (r + 1) * cols, :] = held[i, r].astype(F32)
        marks = jnp.where(meta[0] > 0, seeds[at : at + HALO, :] + 1, 0)
        ref[HALO * cols :, :] = marks.astype(F32)

    @pl.when(meta[1] == 0)
    def _():
        write(near, 1)
        write(far, 0)

    @pl.when(meta[1] != 0)
    def _():
        write(near, 0)
        write(far, 1)


def ends(meta, seeds, feats):
    height, cols, chans = feats.shape
    message = jax.ShapeDtypeStruct((HALO * cols + HALO, chans), F32)
    return pl.pallas_call(
        ends_kernel,
        out_shape=(message, message),
        in_specs=[SMEM, VMEM, ANY],
        out_specs=(VMEM, VMEM),
        scratch_shapes=[
            pltpu.VMEM((2, HALO, cols, chans), BF16),
            pltpu.SemaphoreType.DMA((2,)),
        ],
        compiler_params=params(8),
        cost_estimate=cost(0, 4 << 20),
        name="ends",
    )(meta, seeds, feats)


def side_kernel(meta, seeds, near, far, feats, out, held, marks, sem):
    height, cols, chans = feats.shape
    deep = marks.shape[0]
    width = held.shape[1]
    sub, left = meta[1], meta[2]
    start = pl.multiple_of(jnp.where(left > 0, 0, cols - width), width)
    copy = pltpu.make_async_copy(feats.at[:, pl.ds(start, width), :], held, sem)
    copy.start()
    marks[...] = jnp.zeros_like(marks)
    marks[HALO : HALO + height, :] = jnp.where(meta[0] > 0, seeds[...] + 1, 0).astype(F32)
    low, skip = HALO + height, jnp.where(left > 0, 0, cols - SIDE)
    skip = pl.multiple_of(skip, SIDE)

    def ends_of(ref, at):
        marks[at : at + HALO, :] = ref[HALO * cols :, :]
        for r in range(HALO):
            out[(at + r) * SIDE : (at + r + 1) * SIDE, :] = ref[pl.ds(r * cols + skip, SIDE), :]

    @pl.when(sub == 0)
    def _():
        ends_of(near, low)
        ends_of(far, 0)

    @pl.when(sub != 0)
    def _():
        ends_of(far, low)
        ends_of(near, 0)

    lane = lax.broadcasted_iota(jnp.int32, (cols, LANES), 1)
    source = lax.broadcasted_iota(jnp.int32, (cols, LANES), 0)
    spread = (source == lane % SIDE + skip).astype(BF16)
    spun = jnp.dot(marks[...].astype(BF16), spread, preferred_element_type=F32)
    per = LANES // SIDE
    groups = deep // per
    mine = lax.broadcasted_iota(jnp.int32, (per, LANES), 1) // SIDE
    mine = mine == lax.broadcasted_iota(jnp.int32, (per, LANES), 0)
    out[deep * SIDE :, :] = jnp.zeros((STATS, chans), F32)
    for g in range(groups):
        row = jnp.where(mine, spun[g * per : (g + 1) * per], 0.0)
        out[deep * SIDE + g : deep * SIDE + g + 1, :LANES] = jnp.sum(row, axis=0, keepdims=True)
    out[(height + 2 * HALO) * SIDE : deep * SIDE, :] = jnp.zeros(
        ((deep - height - 2 * HALO) * SIDE, chans), F32
    )
    copy.wait()

    @pl.when(left > 0)
    def _():
        for r in range(height):
            at = (HALO + r) * SIDE
            out[at : at + SIDE, :] = held[r].astype(F32)[:SIDE]

    @pl.when(left == 0)
    def _():
        for r in range(height):
            at = (HALO + r) * SIDE
            out[at : at + SIDE, :] = held[r].astype(F32)[width - SIDE :]


def side(meta, seeds, near, far, feats):
    height, cols, chans = feats.shape
    per = LANES // SIDE
    deep = -(-(height + 2 * HALO) // per) * per
    return pl.pallas_call(
        side_kernel,
        out_shape=jax.ShapeDtypeStruct((deep * SIDE + STATS, chans), F32),
        in_specs=[SMEM, VMEM, VMEM, VMEM, ANY],
        out_specs=VMEM,
        scratch_shapes=[
            pltpu.VMEM((height, 2 * SIDE, chans), BF16),
            pltpu.VMEM((deep, cols), F32),
            pltpu.SemaphoreType.DMA(()),
        ],
        compiler_params=params(8),
        cost_estimate=cost(0, 2 << 20),
        name="side",
    )(meta, seeds, near, far, feats)


def pool_kernel(meta, seeds, feats, protos, keep, give, score, weight, acc, peak, total):
    rows, cols, chans = feats.shape
    count = protos.shape[0]
    classes = count // 4
    step = pl.program_id(0)

    @pl.when(step == 0)
    def _():
        acc[...] = jnp.zeros_like(acc)
        total[...] = jnp.zeros_like(total)
        peak[...] = jnp.full_like(peak, LOW)

    labels = lax.broadcasted_iota(jnp.int32, (classes, cols), 0)
    top = jnp.full((count, LANES), LOW, F32)
    for r in range(rows):
        here = jnp.where(meta[0] > 0, seeds[r : r + 1, :], -1)
        member = here == labels
        raw = lax.dot_general(
            protos[...], feats[r], (((1,), (1,)), ((), ())), preferred_element_type=F32
        )
        masked = jnp.concatenate(
            [
                jnp.where(member, raw[m * classes : (m + 1) * classes], LOW)
                for m in range(count // classes)
            ],
            axis=0,
        )
        score[:, r * cols : (r + 1) * cols] = masked
        for c in range(cols // LANES):
            top = jnp.maximum(top, masked[:, c * LANES : (c + 1) * LANES])
    before = peak[...]
    after = jnp.maximum(before, jnp.max(top, axis=1, keepdims=True))
    fade = jnp.exp(before - after)
    shift = jnp.maximum(after, 0.1 * LOW)
    gained = jnp.zeros((count, LANES), F32)
    for c in range(rows * cols // LANES):
        part = jnp.exp(score[:, c * LANES : (c + 1) * LANES] - shift)
        gained = gained + part
        weight[:, c * LANES : (c + 1) * LANES] = part.astype(BF16)
    peak[...] = after
    total[...] = total[...] * fade + gained
    flat = feats[...].reshape(rows * cols, chans)
    acc[...] = acc[...] * fade[:, :1] + jnp.dot(weight[...], flat, preferred_element_type=F32)

    @pl.when(step == pl.num_programs(0) - 1)
    def _():
        sub = meta[1]
        sums = acc[...].T
        tops = peak[...].T[:1]
        totals = jnp.sum(total[...].T, axis=0, keepdims=True)
        half = count // 2

        def write(ref, second):
            lanes = slice(half, count) if second else slice(0, half)
            ref[:chans, :] = sums[:, lanes]
            ref[chans : chans + 1, :] = tops[:, lanes]
            ref[chans + 1 : chans + 2, :] = totals[:, lanes]
            ref[chans + 2 :, :] = jnp.zeros((STATS - 2, half), F32)

        @pl.when(sub == 0)
        def _():
            write(keep, False)
            write(give, True)

        @pl.when(sub != 0)
        def _():
            write(keep, True)
            write(give, False)


def pool(meta, seeds, feats, protos):
    height, cols, chans = feats.shape
    count = protos.shape[0]
    rows = 8
    piece = jax.ShapeDtypeStruct((chans + STATS, count // 2), F32)
    whole = pl.BlockSpec((chans + STATS, count // 2), lambda i, *_: (0, 0))
    return pl.pallas_call(
        pool_kernel,
        out_shape=(piece, piece),
        grid_spec=pltpu.PrefetchScalarGridSpec(
            num_scalar_prefetch=1,
            grid=(height // rows,),
            in_specs=[
                pl.BlockSpec((rows, cols), lambda i, *_: (i, 0)),
                pl.BlockSpec((rows, cols, chans), lambda i, *_: (i, 0, 0)),
                pl.BlockSpec((count, chans), lambda i, *_: (0, 0)),
            ],
            out_specs=(whole, whole),
            scratch_shapes=[
                pltpu.VMEM((count, rows * cols), F32),
                pltpu.VMEM((count, rows * cols), BF16),
                pltpu.VMEM((count, chans), F32),
                pltpu.VMEM((count, LANES), F32),
                pltpu.VMEM((count, LANES), F32),
            ],
        ),
        compiler_params=pltpu.CompilerParams(vmem_limit_bytes=24 << 20),
        cost_estimate=cost(4 * height * cols * chans * count, height * cols * chans * 2),
        name="pool",
    )(meta, seeds, feats, protos)


def merge_kernel(a, b, out):
    chans = a.shape[0] - STATS
    at, bt = a[chans : chans + 1, :], b[chans : chans + 1, :]
    top = jnp.maximum(at, bt)
    fa, fb = jnp.exp(at - top), jnp.exp(bt - top)
    out[:chans, :] = a[:chans, :] * fa + b[:chans, :] * fb
    out[chans : chans + 1, :] = top
    out[chans + 1 : chans + 2, :] = (
        a[chans + 1 : chans + 2, :] * fa + b[chans + 1 : chans + 2, :] * fb
    )
    out[chans + 2 :, :] = jnp.zeros((STATS - 2, a.shape[1]), F32)


def merge(a, b):
    return pl.pallas_call(
        merge_kernel,
        out_shape=jax.ShapeDtypeStruct(a.shape, F32),
        in_specs=[VMEM, VMEM],
        out_specs=VMEM,
        compiler_params=params(2),
        cost_estimate=cost(3 * a.size, 12 * a.size),
        name="merge",
    )(a, b)


def field_kernel(meta, seeds, keep, got, near, far, *rest, sides):
    strips = rest[:sides]
    (
        taps, feats, refined, out,
        held, base, belief, second, lhs, lhs2, sums, mixed, sem, out_sem,
    ) = rest[sides:]
    height, cols, chans = feats.shape
    count = sums.shape[1]
    classes = count // 4
    sub, odd = meta[1], meta[2]
    groups = sem.shape[0]
    rows = height // groups

    def fetch(i):
        at = pl.ds(i * rows, rows)
        return pltpu.make_async_copy(feats.at[at], held.at[at], sem.at[i])

    for i in range(groups):
        fetch(i).start()

    half = count // 2
    first = pl.multiple_of(sub * half, half)
    other = pl.multiple_of((1 - sub) * half, half)
    sums[:, pl.ds(first, half)] = keep[...]
    sums[:, pl.ds(other, half)] = got[...]
    pooled = sums[:chans, :] / sums[chans + 1 : chans + 2, :]
    length = jnp.sqrt(jnp.sum(pooled * pooled, axis=0, keepdims=True) + 1e-06)
    ready = (pooled / length).T
    for c in range(chans // LANES):
        lanes = slice(c * LANES, (c + 1) * LANES)
        for m in range(4):
            mixed[c, pl.ds(m, classes, stride=4), :] = ready[m * classes : (m + 1) * classes, lanes]
        refined[:, lanes] = mixed[c]
    lead = (ready.astype(BF16).astype(F32) * SCALE).astype(BF16)

    labels = lax.broadcasted_iota(jnp.int32, (classes, 1), 0) + 1
    bonus = math.exp(SEED_REWARD)

    def share(grown):
        norm = jnp.sum(grown, axis=0, keepdims=True)
        return grown * (1.0 / jnp.maximum(norm, 1e-30))

    def unary(tokens, code):
        raw = lax.dot_general(lead, tokens, (((1,), (1,)), ((), ())), preferred_element_type=F32)
        parts = [raw[m * classes : (m + 1) * classes] for m in range(4)]
        top = functools.reduce(jnp.maximum, parts)
        top = jnp.max(top, axis=0, keepdims=True)
        top = jnp.where(code == 0, 1e30, top)
        grown = functools.reduce(jnp.add, [jnp.exp(part - top) for part in parts])
        grown = jnp.where(labels == code, grown * bonus, grown)
        return grown, share(grown)

    near_at = jnp.where(sub == 0, HALO + height, 0)
    far_at = jnp.where(sub == 0, 0, HALO + height)
    for i in range(HALO):
        for ref, at in ((near, near_at), (far, far_at)):
            tokens = ref[i * cols : (i + 1) * cols, :].astype(BF16)
            code = ref[HALO * cols + i : HALO * cols + i + 1, :].astype(jnp.int32)
            grown, early = unary(tokens, code)
            base[at + i, :, :cols] = grown
            belief[at + i, :, :cols] = early

    per = LANES // SIDE
    deep = height + 2 * HALO
    lane = lax.broadcasted_iota(jnp.int32, (classes, LANES), 1)
    for g in range(-(-deep // per)):
        found = []
        for strip in strips:
            tokens = strip[g * LANES : (g + 1) * LANES, :].astype(BF16)
            at = strip.shape[0] - STATS + g
            found.append(unary(tokens, strip[at : at + 1, :LANES].astype(jnp.int32)))
        for r in range(min(per, deep - g * per)):
            row = g * per + r
            for ref, one in ((base, 0), (belief, 1)):
                turn = (LANES - r * SIDE) % LANES
                value = pltpu.roll(found[0][one], turn, 1) if turn else found[0][one]
                if len(found) > 1:
                    turn = (turn + SIDE) % LANES
                    more = pltpu.roll(found[1][one], turn, 1) if turn else found[1][one]
                    value = jnp.where(lane < SIDE, value, more)
                ref[row, :, cols:] = value

    @pl.loop(0, groups)
    def _(i):
        fetch(i).wait()
        marks = jnp.where(meta[0] > 0, seeds[pl.ds(pl.multiple_of(i * rows, rows), rows), :] + 1, 0)
        for j in range(rows):
            row = i * rows + j
            grown, early = unary(held[row], marks[j : j + 1, :])
            base[HALO + row, :, :cols] = grown
            belief[HALO + row, :, :cols] = early

    def mix(source, start, batch, into):
        for k in range(0, classes, 16):
            for c in range(0, cols + LANES, LANES):
                cells = [
                    source[start - REACH + j, k : k + 16, c : c + LANES]
                    for j in range(batch + 2 * REACH)
                ]
                for j in range(batch):
                    tall = TAPS[0] * cells[j + REACH]
                    for d in range(1, REACH + 1):
                        tall = tall + TAPS[d] * (cells[j + REACH - d] + cells[j + REACH + d])
                    high = tall.astype(BF16)
                    low = (tall - high.astype(F32)).astype(BF16)
                    at = slice(j * classes + k, j * classes + k + 16)
                    if c < cols:
                        into[at, c : c + LANES] = high
                        into[at, cols + c : cols + c + LANES] = low
                    else:
                        into[at, 2 * cols : 2 * cols + LANES] = high
                        into[at, 2 * cols + LANES :] = low

    def spread(into, batch, width):
        return jnp.dot(
            into[: batch * classes, :], taps[odd, :, :width], preferred_element_type=F32
        )

    @pl.loop(0, (height + 2 * REACH) // 14)
    def _(i):
        start = REACH + i * 14
        for part, into in ((0, lhs), (7, lhs2)):
            mix(belief, start + part, 7, into)
        for part, into in ((0, lhs), (7, lhs2)):
            message = spread(into, 7, cols + LANES)
            for j in range(7):
                row = start + part + j
                sent = message[j * classes : (j + 1) * classes, :] - belief[row]
                second[row] = share(base[row] * jnp.exp(sent))

    def leave(row):
        return pltpu.make_async_copy(
            belief.at[row, :, pl.ds(0, cols)], out.at[:, row, :], out_sem.at[row]
        )

    @pl.loop(0, height // 8)
    def _(i):
        start = HALO + i * 8
        for part, into in ((0, lhs), (4, lhs2)):
            mix(second, start + part, 4, into)
        for part, into in ((0, lhs), (4, lhs2)):
            message = spread(into, 4, cols)
            for j in range(4):
                row = start + part + j
                sent = message[j * classes : (j + 1) * classes, :] - second[row, :, :cols]
                belief[row - HALO, :, :cols] = share(base[row, :, :cols] * jnp.exp(sent))
        for j in range(8):
            leave(i * 8 + j).start()

    @pl.loop(0, height)
    def _(i):
        leave(i).wait()


def field(meta, seeds, keep, got, near, far, strips, feats, count):
    height, cols, chans = feats.shape
    classes = count // 4
    wide = cols + LANES
    deep = height + 2 * HALO
    plane = pltpu.VMEM((deep, classes, wide), F32)
    return pl.pallas_call(
        functools.partial(field_kernel, sides=len(strips)),
        out_shape=(
            jax.ShapeDtypeStruct((count, chans), F32),
            jax.ShapeDtypeStruct((classes, height, cols), F32),
        ),
        in_specs=[SMEM] + [VMEM] * (6 + len(strips)) + [ANY],
        out_specs=(VMEM, ANY),
        scratch_shapes=[
            pltpu.VMEM((height, cols, chans), BF16),
            plane,
            plane,
            plane,
            pltpu.VMEM((8 * classes, 2 * wide), BF16),
            pltpu.VMEM((8 * classes, 2 * wide), BF16),
            pltpu.VMEM((chans + STATS, count), F32),
            pltpu.VMEM((chans // LANES, count, LANES), F32),
            pltpu.SemaphoreType.DMA((8,)),
            pltpu.SemaphoreType.DMA((height,)),
        ],
        compiler_params=params(44),
        cost_estimate=cost(8 * height * cols * chans * count, 16 << 20),
        name="field",
    )(meta, seeds, keep, got, near, far, *strips, jnp.asarray(across_taps(cols, len(strips)), BF16), feats)


def swap(x, axes, pairs):
    return lax.ppermute(x, axes, [p for a, b in pairs for p in ((a, b), (b, a))])


def on_device(features, seeds, valid_tiles, prototypes):
    height, cols, chans = features.shape
    classes, modes, _ = prototypes.shape
    count = classes * modes
    n_row, n_col = lax.axis_size("row"), lax.axis_size("col")
    sub, odd = lax.axis_index("sub"), lax.axis_index("col") % 2
    meta = jnp.stack([valid_tiles[0, 0], sub, odd]).astype(jnp.int32)
    protos = (SCALE * prototypes.astype(F32)).astype(BF16)
    protos = protos.transpose(1, 0, 2).reshape(count, chans)

    near, far = ends(meta, seeds, features)
    far = swap(far, ("row", "sub"), [(2 * i + 1, 2 * i + 2) for i in range(n_row - 1)])
    near = swap(near, "sub", [(0, 1)])

    keep, give = pool(meta, seeds, features, protos)
    keep = merge(keep, swap(give, "sub", [(0, 1)]))

    def doubled(keep, axis, size):
        stride = 1
        while stride < size:
            pairs = [(i, i | stride) for i in range(size) if not i & stride]
            keep = merge(keep, swap(keep, axis, pairs))
            stride *= 2
        return keep

    keep = doubled(keep, "col", n_col)
    keep, near, far = lax.optimization_barrier((keep, near, far))
    strips = [
        swap(
            side(meta, seeds, near, far, features),
            "col",
            [(i, i + 1) for i in range(0, n_col - 1, 2)],
        )
    ]
    if n_col > 2:
        other = jnp.stack([meta[0], meta[1], 1 - odd])
        strips.append(
            swap(
                side(other, seeds, near, far, features),
                "col",
                [(i, i + 1) for i in range(1, n_col - 1, 2)],
            )
        )
    keep = doubled(keep, "row", n_row)
    got = swap(keep, "sub", [(0, 1)])
    refined, belief = field(meta, seeds, keep, got, near, far, strips, features, count)
    return refined.reshape(classes, modes, chans), belief


def solution(mesh):
    placed = (
        P(("groups", "row", "sub"), "col", None),
        P(("groups", "row", "sub"), "col"),
        P(("groups", "row"), "col"),
        P("groups", None, None),
    )
    return jax.shard_map(
        on_device,
        mesh=mesh,
        in_specs=placed,
        out_specs=(P("groups", None, None), P("groups", ("row", "sub"), "col")),
        check_vma=False,
    )
```

time: 113 us -> 77.4 us (0.68)
  Pallas kernels: 65.3 us -> 41 us
  local copies, waits for them, and re-layouts: 13.5 us -> 5.03 us
  other arithmetic: 7.1 us -> 1.14 us
  waiting for transfers between devices: 12.9 us -> 15.8 us
    pallas_call x1 -> x3, Pallas kernels: 43.1 us -> 25.2 us  [the longest x1 23.4 us: field(): pl.pallas_call(functools.partial(field_kernel, sides=len(strips)), out_sh...]
    pallas_call x4, Pallas kernels: 6.59 us -> 0.11 us  [merge(): pl.pallas_call(merge_kernel, out_shape=jax.ShapeDtypeStruct(a.shape, F32)...]
    concatenate x6 -> x0, other arithmetic: 3.72 us -> none  [the longest x2 2.51 us: edge_rows(): jnp.concatenate([rows.reshape(-1, chans), marks.reshape(-1, chans)], axis=0)]
    slice x8 -> x0, local copies, waits for them, and re-layouts: 3.53 us -> none  [the longest x3 2.77 us: cut(): rows = msg[:HALO * cols].reshape(HALO, cols, chans)]
    ppermute x8, waiting for transfers between devices: 12.9 us -> 15.8 us  [swap(): lax.ppermute(x, axes, [p for a, b in pairs for p in ((a, b), (b, a))])]
    select_n x4 -> x0, other arithmetic: 1.81 us -> none  [the longest x2 0.89 us: edge_cols(): jnp.where(sub == 0, f, n)]
    reshape x10 -> x0, local copies, waits for them, and re-layouts: 1.49 us -> none  [the longest x1 0.67 us: on_device(): marks = jnp.pad(marks, ((0, more[0]), (0, more[1]))).reshape(-1, LANES)]
    dynamic_slice x1 -> x0, local copies, waits for them, and re-layouts: 1.49 us -> none  [edge_rows(): rows = lax.dynamic_slice_in_dim(features, start, HALO, axis=0).astype(F32)]
  transfers between devices with their start and end apart: 8 -> 8, of which waited for: 4 -> 6; matrix products, arithmetic and copies ran while one was open for 5% -> 1% of each run, Pallas kernels for 20% -> 21%
where the time goes in v1:
time: 77.4 us; the launch traced here: 77.2 us
  Pallas kernels  41 us (53%)
  waiting for transfers between devices  15.8 us (20%)
  starting transfers between devices  12.8 us (17%)
  local copies, waits for them, and re-layouts  5.03 us (6%)
  between operations  1.42 us (2%)
  other arithmetic  1.14 us (1%)
    pallas_call x1, Pallas kernels, field(): pl.pallas_call(functools.partial(field_kernel, sides=len(strips)), out_sh...  23.4 us
    ppermute x8, waiting for transfers between devices, swap(): lax.ppermute(x, axes, [p for a, b in pairs for p in ((a, b), (b, a))])  15.8 us
    pallas_call x1, Pallas kernels, pool(): pl.pallas_call(pool_kernel, out_shape=(piece, piece), grid_spec=pltpu.Pre...  15.7 us
    ppermute x8, starting transfers between devices, swap(): lax.ppermute(x, axes, [p for a, b in pairs for p in ((a, b), (b, a))])  12.8 us
    unnamed x10, local copies, waits for them, and re-layouts  4.24 us
  transfers between devices with their start and end apart: 8, of which 6 were waited for; matrix products, arithmetic and copies ran while one was open for 1% of the time, Pallas kernels for 21%

profile of v1, /device:TPU:0, one launch (start us, length us, event | category | flops | bytes accessed | tf_op | source)
XLA Modules:
  0.0 77.2 jit_solution(4095742782204624650)
XLA Ops:
  1.3 0.1 pad_add_fusion.meta
  1.4 3.4 %copy-done = bf16[64,256,256]{2,1,0:T(8,128)(2,1)S(1)} copy-done((bf16[64,256,256]{2,1,0:T(8,128)(2,1)S(1)}, bf16[64,256,256]{2,1,0:T(8,128)(2,1)}, u32[]{:S(2)}) %copy-start) | copy-done | bytes 8388632
  4.7 0.8 %copy-done.2 = s32[64,256]{1,0:T(8,128)S(1)} copy-done((s32[64,256]{1,0:T(8,128)S(1)}, s32[64,256]{1,0:T(8,128)}, u32[]{:S(2)}) %copy-start.2) | copy-done | bytes 65560
  5.6 0.9 %ends.1 = (f32[1542,256]{1,0:T(8,128)S(1)}, f32[1542,256]{1,0:T(8,128)S(1)}) custom-call(s32[3]{0:T(128)S(1)} %pad_add_fusion.meta, s32[64,256]{1,0:T(8,128)S(1)} %copy-done.2, bf16[64,256,256]{2,1,0:T(8,128)(2,1)S(1)} %copy-done), custom_call_target="tpu_custom_call" | custom-call | bytes 4194304 | tf_op jit(solution)/shard_map/ends/pallas_call | solution.py:87
  6.5 0.5 collective-permute-start.2
  7.0 0.9 %collective-permute-start.3 = (f32[1542,256]{1,0:T(8,128)S(1)}, f32[1542,256]{1,0:T(8,128)S(1)}, u32[]{:S(2)}, u32[]{:S(2)}) collective-permute-start(f32[1542,256]{1,0:T(8,128)S(1)} %get-tuple-element.14), channel_id=1, source_target_pairs={{1,4},{4,1},{5,8},{8,5},{9,12},{12,9},{3,6},{6,3},{7,10},{10,7},{1... | collective-permute-start | bytes 4737032 | tf_op jit(solution)/shard_map/ppermute | solution.py:494
  7.9 1.1 %fusion = bf16[4,64,256]{2,0,1:T(4,128)(2,1)S(1)} fusion(bf16[64,4,256]{2,1,0:T(4,128)(2,1)} %param.8), kind=kLoop, calls=%fused_computation.1 | loop fusion | flops 196608 | bytes 262144 | tf_op jit(solution)/shard_map/transpose | solution.py:505
  9.0 15.7 %pool.1 = (f32[264,128]{1,0:T(8,128)S(1)}, f32[264,128]{1,0:T(8,128)S(1)}) custom-call(s32[3]{0:T(128)S(1)} %pad_add_fusion.meta, s32[64,256]{1,0:T(8,128)S(1)} %copy-done.3, bf16[64,256,256]{2,1,0:T(8,128)(2,1)S(1)} %copy-done.1, bf16[256,256]{1,0:T(8,128)(2,1)S(1)} %bitcast.7), custom_call_target="tpu_custom_call" | custom-call | flops 4294967296 | bytes 8388608 | tf_op jit(solution)/shard_map/pool/pallas_call | solution.py:256
  24.7 4.0 %collective-permute-start = (f32[264,128]{1,0:T(8,128)S(1)}, f32[264,128]{1,0:T(8,128)S(1)}, u32[]{:S(2)}, u32[]{:S(2)}) collective-permute-start(f32[264,128]{1,0:T(8,128)S(1)} %get-tuple-element.12), channel_id=1, source_target_pairs={{0,1},{1,0},{2,3},{3,2},{4,5},{5,4},{6,7},{7,6},{8,9},{9,8},{10,11... | collective-permute-start | bytes 405512 | tf_op jit(solution)/shard_map/ppermute | solution.py:494
  28.7 1.0 %collective-permute-done.b = f32[264,128]{1,0:T(8,128)S(1)} collective-permute-done((f32[264,128]{1,0:T(8,128)S(1)}, f32[264,128]{1,0:T(8,128)S(1)}, u32[]{:S(2)}, u32[]{:S(2)}) %collective-permute-start) | collective-permute-done | bytes 135200 | tf_op jit(solution)/shard_map/ppermute | solution.py:494
  29.7 1.6 %collective-permute-start.1 = (f32[264,128]{1,0:T(8,128)S(1)}, f32[264,128]{1,0:T(8,128)S(1)}, u32[]{:S(2)}, u32[]{:S(2)}) collective-permute-start(f32[264,128]{1,0:T(8,128)S(1)} %merge.4.a), channel_id=1, source_target_pairs={{0,2},{2,0},{1,3},{3,1},{4,6},{6,4},{5,7},{7,5},{8,10},{10,8},{9,1... | collective-permute-start | bytes 405512 | tf_op jit(solution)/shard_map/ppermute | solution.py:494
  31.3 4.3 %collective-permute-done.1.b = f32[264,128]{1,0:T(8,128)S(1)} collective-permute-done((f32[264,128]{1,0:T(8,128)S(1)}, f32[264,128]{1,0:T(8,128)S(1)}, u32[]{:S(2)}, u32[]{:S(2)}) %collective-permute-start.1) | collective-permute-done | bytes 135200 | tf_op jit(solution)/shard_map/ppermute | solution.py:494
  35.7 0.0 copy-start.4
  35.7 0.8 %side.1 = f32[648,256]{1,0:T(8,128)S(1)} custom-call(s32[3]{0:T(128)S(1)} %pad_add_fusion.meta, s32[64,256]{1,0:T(8,128)S(1)} %copy-done.3, f32[1542,256]{1,0:T(8,128)S(1)} %collective-permute-done.2.near, f32[1542,256]{1,0:T(8,128)S(1)} %collective-permute-done.3.far, bf16[64,256,256]{2,1,0:T(8,128)(2,1)S(1)} %copy-done.1), custom_call_target="tpu_custom_call" | custom-call | bytes 2097152 | tf_op jit(solution)/shard_map/side/pallas_call | solution.py:164
  36.6 1.6 %collective-permute-start.7 = (f32[648,256]{1,0:T(8,128)S(1)}, f32[648,256]{1,0:T(8,128)S(1)}, u32[]{:S(2)}, u32[]{:S(2)}) collective-permute-start(f32[648,256]{1,0:T(8,128)S(1)} %side.1), channel_id=1, source_target_pairs={{0,2},{2,0},{1,3},{3,1},{4,6},{6,4},{5,7},{7,5},{8,10},{10,8},{9,1... | collective-permute-start | bytes 1990664 | tf_op jit(solution)/shard_map/ppermute | solution.py:494
  38.1 1.6 %collective-permute-start.4 = (f32[264,128]{1,0:T(8,128)S(1)}, f32[264,128]{1,0:T(8,128)S(1)}, u32[]{:S(2)}, u32[]{:S(2)}) collective-permute-start(f32[264,128]{1,0:T(8,128)S(1)} %merge.5.a), channel_id=1, source_target_pairs={{0,4},{4,0},{8,12},{12,8},{1,5},{5,1},{9,13},{13,9},{2,6},{6,2},{1... | collective-permute-start | bytes 405512 | tf_op jit(solution)/shard_map/ppermute | solution.py:494
  39.7 3.4 %collective-permute-done.4.b = f32[264,128]{1,0:T(8,128)S(1)} collective-permute-done((f32[264,128]{1,0:T(8,128)S(1)}, f32[264,128]{1,0:T(8,128)S(1)}, u32[]{:S(2)}, u32[]{:S(2)}) %collective-permute-start.4) | collective-permute-done | bytes 135200 | tf_op jit(solution)/shard_map/ppermute | solution.py:494
  43.2 2.7 %collective-permute-start.5 = (f32[264,128]{1,0:T(8,128)S(1)}, f32[264,128]{1,0:T(8,128)S(1)}, u32[]{:S(2)}, u32[]{:S(2)}) collective-permute-start(f32[264,128]{1,0:T(8,128)S(1)} %merge.6.a), channel_id=1, source_target_pairs={{0,8},{8,0},{4,12},{12,4},{1,9},{9,1},{5,13},{13,5},{2,10},{10,2},... | collective-permute-start | bytes 405512 | tf_op jit(solution)/shard_map/ppermute | solution.py:494
  45.8 5.1 %collective-permute-done.5.b = f32[264,128]{1,0:T(8,128)S(1)} collective-permute-done((f32[264,128]{1,0:T(8,128)S(1)}, f32[264,128]{1,0:T(8,128)S(1)}, u32[]{:S(2)}, u32[]{:S(2)}) %collective-permute-start.5) | collective-permute-done | bytes 135200 | tf_op jit(solution)/shard_map/ppermute | solution.py:494
  51.0 0.1 collective-permute-start.6
  51.0 1.3 %collective-permute-done.6.got = f32[264,128]{1,0:T(8,128)S(1)} collective-permute-done((f32[264,128]{1,0:T(8,128)S(1)}, f32[264,128]{1,0:T(8,128)S(1)}, u32[]{:S(2)}, u32[]{:S(2)}) %collective-permute-start.6) | collective-permute-done | bytes 135200 | tf_op jit(solution)/shard_map/ppermute | solution.py:494
  52.4 0.6 collective-permute-done.7.rest_0_
  53.0 23.4 %field.1 = (f32[256,256]{1,0:T(8,128)S(1)}, f32[64,64,256]{2,1,0:T(8,128)}) custom-call(s32[3]{0:T(128)S(1)} %pad_add_fusion.meta, s32[64,256]{1,0:T(8,128)S(1)} %copy-done.3, f32[264,128]{1,0:T(8,128)S(1)} %merge.7.keep, f32[264,128]{1,0:T(8,128)S(1)} %collective-permute-done.6.got, f32[1542,256]{1,0:T(8,128)S(1)} %collective-permute-done.2.near, ...), custom_call_target="tpu_custom_call" | custom-call | flops 8589934592 | bytes 16777216 | tf_op jit(solution)/shard_map/field/pallas_call | solution.py:467
  76.4 0.8 %reshape.11 = f32[64,4,256]{2,1,0:T(4,128)} reshape(f32[256,256]{1,0:T(8,128)S(1)} %get-tuple-element.18) | data formatting | bytes 524288 | tf_op jit(solution)/shard_map/reshape | solution.py:543
  (14 shorter events, 0.1 us)
Async XLA Ops:
  1.4 3.4 %copy-start = (bf16[64,256,256]{2,1,0:T(8,128)(2,1)S(1)}, bf16[64,256,256]{2,1,0:T(8,128)(2,1)}, u32[]{:S(2)}) copy-start(bf16[64,256,256]{2,1,0:T(8,128)(2,1)} %rest_2_.1) | copy-start | bytes 25165828
  4.7 0.8 %copy-start.2 = (s32[64,256]{1,0:T(8,128)S(1)}, s32[64,256]{1,0:T(8,128)}, u32[]{:S(2)}) copy-start(s32[64,256]{1,0:T(8,128)} %seeds.7) | copy-start | bytes 196612
  5.6 3.4 %copy-start.1 = (bf16[64,256,256]{2,1,0:T(8,128)(2,1)S(1)}, bf16[64,256,256]{2,1,0:T(8,128)(2,1)}, u32[]{:S(2)}) copy-start(bf16[64,256,256]{2,1,0:T(8,128)(2,1)} %rest_2_.1) | copy-start | bytes 25165828
  5.6 3.4 %copy-start.3 = (s32[64,256]{1,0:T(8,128)S(1)}, s32[64,256]{1,0:T(8,128)}, u32[]{:S(2)}) copy-start(s32[64,256]{1,0:T(8,128)} %seeds.7) | copy-start | bytes 196612
  6.5 29.2 %collective-permute-start.2 = (f32[1542,256]{1,0:T(8,128)S(1)}, f32[1542,256]{1,0:T(8,128)S(1)}, u32[]{:S(2)}, u32[]{:S(2)}) collective-permute-start(f32[1542,256]{1,0:T(8,128)S(1)} %get-tuple-element.13), channel_id=1, source_target_pairs={{0,1},{1,0},{2,3},{3,2},{4,5},{5,4},{6,7},{7,6},{8,9},{9,8},{10,11... | collective-permute-start | bytes 4737032 | tf_op jit(solution)/shard_map/ppermute | solution.py:494
  7.0 28.7 %collective-permute-start.3 = (f32[1542,256]{1,0:T(8,128)S(1)}, f32[1542,256]{1,0:T(8,128)S(1)}, u32[]{:S(2)}, u32[]{:S(2)}) collective-permute-start(f32[1542,256]{1,0:T(8,128)S(1)} %get-tuple-element.14), channel_id=1, source_target_pairs={{1,4},{4,1},{5,8},{8,5},{9,12},{12,9},{3,6},{6,3},{7,10},{10,7},{1... | collective-permute-start | bytes 4737032 | tf_op jit(solution)/shard_map/ppermute | solution.py:494
  24.7 5.0 %collective-permute-start = (f32[264,128]{1,0:T(8,128)S(1)}, f32[264,128]{1,0:T(8,128)S(1)}, u32[]{:S(2)}, u32[]{:S(2)}) collective-permute-start(f32[264,128]{1,0:T(8,128)S(1)} %get-tuple-element.12), channel_id=1, source_target_pairs={{0,1},{1,0},{2,3},{3,2},{4,5},{5,4},{6,7},{7,6},{8,9},{9,8},{10,11... | collective-permute-start | bytes 405512 | tf_op jit(solution)/shard_map/ppermute | solution.py:494
  29.7 5.9 %collective-permute-start.1 = (f32[264,128]{1,0:T(8,128)S(1)}, f32[264,128]{1,0:T(8,128)S(1)}, u32[]{:S(2)}, u32[]{:S(2)}) collective-permute-start(f32[264,128]{1,0:T(8,128)S(1)} %merge.4.a), channel_id=1, source_target_pairs={{0,2},{2,0},{1,3},{3,1},{4,6},{6,4},{5,7},{7,5},{8,10},{10,8},{9,1... | collective-permute-start | bytes 405512 | tf_op jit(solution)/shard_map/ppermute | solution.py:494
  35.7 17.3 %copy-start.4 = (bf16[2,768,384]{2,1,0:T(8,128)(2,1)S(1)}, bf16[2,768,384]{2,1,0:T(8,128)(2,1)}, u32[]{:S(2)}) copy-start(bf16[2,768,384]{2,1,0:T(8,128)(2,1)} %constant.23.clone.rest_1_) | copy-start | bytes 3538948
  36.6 16.4 %collective-permute-start.7 = (f32[648,256]{1,0:T(8,128)S(1)}, f32[648,256]{1,0:T(8,128)S(1)}, u32[]{:S(2)}, u32[]{:S(2)}) collective-permute-start(f32[648,256]{1,0:T(8,128)S(1)} %side.1), channel_id=1, source_target_pairs={{0,2},{2,0},{1,3},{3,1},{4,6},{6,4},{5,7},{7,5},{8,10},{10,8},{9,1... | collective-permute-start | bytes 1990664 | tf_op jit(solution)/shard_map/ppermute | solution.py:494
  38.1 5.0 %collective-permute-start.4 = (f32[264,128]{1,0:T(8,128)S(1)}, f32[264,128]{1,0:T(8,128)S(1)}, u32[]{:S(2)}, u32[]{:S(2)}) collective-permute-start(f32[264,128]{1,0:T(8,128)S(1)} %merge.5.a), channel_id=1, source_target_pairs={{0,4},{4,0},{8,12},{12,8},{1,5},{5,1},{9,13},{13,9},{2,6},{6,2},{1... | collective-permute-start | bytes 405512 | tf_op jit(solution)/shard_map/ppermute | solution.py:494
  43.2 7.8 %collective-permute-start.5 = (f32[264,128]{1,0:T(8,128)S(1)}, f32[264,128]{1,0:T(8,128)S(1)}, u32[]{:S(2)}, u32[]{:S(2)}) collective-permute-start(f32[264,128]{1,0:T(8,128)S(1)} %merge.6.a), channel_id=1, source_target_pairs={{0,8},{8,0},{4,12},{12,4},{1,9},{9,1},{5,13},{13,5},{2,10},{10,2},... | collective-permute-start | bytes 405512 | tf_op jit(solution)/shard_map/ppermute | solution.py:494
  51.0 1.4 %collective-permute-start.6 = (f32[264,128]{1,0:T(8,128)S(1)}, f32[264,128]{1,0:T(8,128)S(1)}, u32[]{:S(2)}, u32[]{:S(2)}) collective-permute-start(f32[264,128]{1,0:T(8,128)S(1)} %merge.7.keep), channel_id=1, source_target_pairs={{0,1},{1,0},{2,3},{3,2},{4,5},{5,4},{6,7},{7,6},{8,9},{9,8},{10,11... | collective-permute-start | bytes 405512 | tf_op jit(solution)/shard_map/ppermute | solution.py:494

commit v2 on v1

v2 whole, which is shorter than its diff:
```python
import functools
import math

import jax
import jax.numpy as jnp
import numpy as np
from jax import lax
from jax.experimental import pallas as pl
from jax.experimental.pallas import tpu as pltpu
from jax.sharding import PartitionSpec as P

ITERS = 2
SCALE = 2.0
SEED_REWARD = 2.0
LOW = -1e30
REACH = 3
HALO = ITERS * REACH
LANES = 128
STATS = 8
SIDE = 8
EDGE = 32
CHUNKS = 1
GAIN = 1.461325
TAPS = [math.exp(-(d * d) / 8.0) / GAIN for d in range(REACH + 1)]
F32 = jnp.float32
BF16 = jnp.bfloat16
VMEM = pl.BlockSpec(memory_space=pltpu.VMEM)
SMEM = pl.BlockSpec(memory_space=pltpu.SMEM)
ANY = pl.BlockSpec(memory_space=pl.ANY)
HBM = pl.BlockSpec(memory_space=pltpu.HBM)


def cost(flops, moved):
    return pl.CostEstimate(flops=flops, bytes_accessed=moved, transcendentals=0)


def params(mib):
    return pltpu.CompilerParams(vmem_limit_bytes=mib << 20)


def in_hbm(x):
    return pltpu.with_memory_space_constraint(x, pltpu.HBM)


def across_taps(cols, sides):
    nowhere = -(10**6)

    def stencil(source, target):
        gap = np.abs(source[:, None] - target[None, :])
        used = (source[:, None] != nowhere) & (target[None, :] != nowhere) & (gap <= REACH)
        return np.where(used, GAIN * np.exp(-np.minimum(gap, REACH) ** 2 / 8.0), 0.0)

    both = []
    for odd in (False, True):
        own = np.arange(cols)
        packed = np.full(LANES, nowhere)
        right, left = (EDGE + SIDE, EDGE) if odd else (EDGE, EDGE + SIDE)
        if sides == 2 or not odd:
            packed[right : right + HALO] = cols + np.arange(HALO)
        if sides == 2 or odd:
            packed[left + SIDE - HALO : left + SIDE] = np.arange(-HALO, 0)
        full = packed.copy()
        full[:EDGE] = own[:EDGE]
        full[LANES - EDGE :] = own[cols - EDGE :]
        main = stencil(own, own)
        near = stencil(packed, own)
        side = stencil(full, packed)
        none = np.zeros((cols, LANES))
        both.append(
            np.block([[main, none], [main, none], [near, side], [near, side]])
        )
    return np.stack(both)


def ends_kernel(meta, seeds, feats, near, far, held, labels, sem):
    height, cols, chans = feats.shape
    fetch = [
        pltpu.make_async_copy(feats.at[pl.ds(at, HALO)], held.at[i], sem.at[i])
        for i, at in enumerate((0, height - HALO))
    ] + [
        pltpu.make_async_copy(seeds.at[pl.ds(at, 8)], labels.at[i], sem.at[2 + i])
        for i, at in enumerate((0, height - 8))
    ]
    for copy in fetch:
        copy.start()
    for copy in fetch:
        copy.wait()

    def write(ref, i):
        at = (0, 8 - HALO)[i]
        for r in range(HALO):
            ref[r * cols : (r + 1) * cols, :] = held[i, r].astype(F32)
        marks = jnp.where(meta[0] > 0, labels[i, at : at + HALO, :] + 1, 0)
        ref[HALO * cols :, :] = marks.astype(F32)

    @pl.when(meta[1] == 0)
    def _():
        write(near, 1)
        write(far, 0)

    @pl.when(meta[1] != 0)
    def _():
        write(near, 0)
        write(far, 1)


def ends(meta, seeds, feats):
    height, cols, chans = feats.shape
    message = jax.ShapeDtypeStruct((HALO * cols + HALO, chans), F32)
    return pl.pallas_call(
        ends_kernel,
        out_shape=(message, message),
        in_specs=[SMEM, HBM, HBM],
        out_specs=(VMEM, VMEM),
        scratch_shapes=[
            pltpu.VMEM((2, HALO, cols, chans), BF16),
            pltpu.VMEM((2, 8, cols), jnp.int32),
            pltpu.SemaphoreType.DMA((4,)),
        ],
        compiler_params=params(8),
        cost_estimate=cost(0, 4 << 20),
        name="ends",
    )(meta, in_hbm(seeds), in_hbm(feats))


def side_kernel(meta, seeds, near, far, feats, out, marks):
    height, cols, chans = feats.shape
    deep = marks.shape[0]
    width = 2 * SIDE
    sub, left = meta[1], meta[2]
    marks[...] = jnp.zeros_like(marks)
    marks[HALO : HALO + height, :] = jnp.where(meta[0] > 0, seeds[...] + 1, 0).astype(F32)
    low, skip = HALO + height, jnp.where(left > 0, 0, cols - SIDE)
    skip = pl.multiple_of(skip, SIDE)

    def ends_of(ref, at):
        marks[at : at + HALO, :] = ref[HALO * cols :, :]
        for r in range(HALO):
            out[(at + r) * SIDE : (at + r + 1) * SIDE, :] = ref[pl.ds(r * cols + skip, SIDE), :]

    @pl.when(sub == 0)
    def _():
        ends_of(near, low)
        ends_of(far, 0)

    @pl.when(sub != 0)
    def _():
        ends_of(far, low)
        ends_of(near, 0)

    lane = lax.broadcasted_iota(jnp.int32, (cols, LANES), 1)
    source = lax.broadcasted_iota(jnp.int32, (cols, LANES), 0)
    spread = (source == lane % SIDE + skip).astype(BF16)
    spun = jnp.dot(marks[...].astype(BF16), spread, preferred_element_type=F32)
    per = LANES // SIDE
    groups = deep // per
    mine = lax.broadcasted_iota(jnp.int32, (per, LANES), 1) // SIDE
    mine = mine == lax.broadcasted_iota(jnp.int32, (per, LANES), 0)
    out[deep * SIDE :, :] = jnp.zeros((STATS, chans), F32)
    for g in range(groups):
        row = jnp.where(mine, spun[g * per : (g + 1) * per], 0.0)
        out[deep * SIDE + g : deep * SIDE + g + 1, :LANES] = jnp.sum(row, axis=0, keepdims=True)
    out[(height + 2 * HALO) * SIDE : deep * SIDE, :] = jnp.zeros(
        ((deep - height - 2 * HALO) * SIDE, chans), F32
    )

    @pl.when(left > 0)
    def _():
        for r in range(height):
            at = (HALO + r) * SIDE
            out[at : at + SIDE, :] = feats[r, :width].astype(F32)[:SIDE]

    @pl.when(left == 0)
    def _():
        for r in range(height):
            at = (HALO + r) * SIDE
            out[at : at + SIDE, :] = feats[r, cols - width :].astype(F32)[SIDE:]


def side(meta, seeds, near, far, feats):
    height, cols, chans = feats.shape
    per = LANES // SIDE
    deep = -(-(height + 2 * HALO) // per) * per
    return pl.pallas_call(
        side_kernel,
        out_shape=jax.ShapeDtypeStruct((deep * SIDE + STATS, chans), F32),
        in_specs=[SMEM, VMEM, VMEM, VMEM, VMEM],
        out_specs=VMEM,
        scratch_shapes=[pltpu.VMEM((deep, cols), F32)],
        compiler_params=params(8),
        cost_estimate=cost(0, 2 << 20),
        name="side",
    )(meta, seeds, near, far, feats)


def pool_kernel(meta, seeds, feats, given, *rest, rows):
    keep, give, scratch = rest[:CHUNKS], rest[CHUNKS : 2 * CHUNKS], rest[2 * CHUNKS :]
    score, weight, top = scratch[:2], scratch[2:4], scratch[4:6]
    acc, peak, total, protos = scratch[6:]
    height, cols, chans = feats.shape
    classes, modes, _ = given.shape
    count = classes * modes
    wide = given[...].astype(F32) * SCALE
    for m in range(modes):
        protos[m * classes : (m + 1) * classes, :] = wide[:, m, :].astype(BF16)
    chunks = height // rows
    acc[...] = jnp.zeros_like(acc)
    total[...] = jnp.zeros_like(total)
    peak[...] = jnp.full_like(peak, LOW)
    labels = lax.broadcasted_iota(jnp.int32, (classes, cols), 0)

    def rate(chunk, slot):
        best = jnp.full((count, LANES), LOW, F32)
        for r in range(rows):
            here = jnp.where(meta[0] > 0, seeds[pl.ds(chunk * rows + r, 1), :], -1)
            member = here == labels
            raw = lax.dot_general(
                protos[...],
                feats[chunk * rows + r],
                (((1,), (1,)), ((), ())),
                preferred_element_type=F32,
            )
            masked = jnp.concatenate(
                [
                    jnp.where(member, raw[m * classes : (m + 1) * classes], LOW)
                    for m in range(count // classes)
                ],
                axis=0,
            )
            score[slot][:, r * cols : (r + 1) * cols] = masked
            for c in range(cols // LANES):
                best = jnp.maximum(best, masked[:, c * LANES : (c + 1) * LANES])
        top[slot][...] = best

    def gather(chunk, slot):
        before = peak[...]
        after = jnp.maximum(before, jnp.max(top[slot][...], axis=1, keepdims=True))
        fade = jnp.exp(before - after)
        shift = jnp.maximum(after, 0.1 * LOW)
        gained = jnp.zeros((count, LANES), F32)
        for c in range(rows * cols // LANES):
            part = jnp.exp(score[slot][:, c * LANES : (c + 1) * LANES] - shift)
            gained = gained + part
            weight[slot][:, c * LANES : (c + 1) * LANES] = part.astype(BF16)
        peak[...] = after
        total[...] = total[...] * fade + gained
        flat = feats[pl.ds(chunk * rows, rows)].reshape(rows * cols, chans)
        grown = jnp.dot(weight[slot][...], flat, preferred_element_type=F32)
        for c in range(chans // LANES):
            lanes = slice(c * LANES, (c + 1) * LANES)
            acc[:, lanes] = acc[:, lanes] * fade + grown[:, lanes]

    rate(0, 0)

    @pl.loop(0, chunks // 2)
    def _(i):
        rate(2 * i + 1, 1)
        gather(2 * i, 0)
        rate(jnp.minimum(2 * i + 2, chunks - 1), 0)
        gather(2 * i + 1, 1)

    sub = meta[1]
    sums = acc[...].T
    tops = peak[...].T[:1]
    totals = jnp.sum(total[...].T, axis=0, keepdims=True)
    half = count // 2

    part = chans // CHUNKS

    def write(refs, second):
        lanes = slice(half, count) if second else slice(0, half)
        for i, ref in enumerate(refs):
            ref[:part, :] = sums[i * part : (i + 1) * part, lanes]
            ref[part : part + 1, :] = tops[:, lanes]
            ref[part + 1 : part + 2, :] = totals[:, lanes]
            ref[part + 2 :, :] = jnp.zeros((STATS - 2, half), F32)

    @pl.when(sub == 0)
    def _():
        write(keep, False)
        write(give, True)

    @pl.when(sub != 0)
    def _():
        write(keep, True)
        write(give, False)


def pool(meta, seeds, feats, protos):
    height, cols, chans = feats.shape
    count = protos.shape[0] * protos.shape[1]
    rows = 4
    piece = jax.ShapeDtypeStruct((chans // CHUNKS + STATS, count // 2), F32)
    flat = (count, rows * cols)
    narrow = pltpu.VMEM((count, LANES), F32)
    out = pl.pallas_call(
        functools.partial(pool_kernel, rows=rows),
        out_shape=(piece,) * (2 * CHUNKS),
        in_specs=[SMEM, VMEM, VMEM, VMEM],
        out_specs=(VMEM,) * (2 * CHUNKS),
        scratch_shapes=[pltpu.VMEM(flat, F32)] * 2
        + [pltpu.VMEM(flat, BF16)] * 2
        + [narrow] * 2
        + [pltpu.VMEM((count, chans), F32), narrow, narrow, pltpu.VMEM((count, chans), BF16)],
        compiler_params=params(8),
        cost_estimate=cost(4 * height * cols * chans * count, height * cols * chans * 2),
        name="pool",
    )(meta, seeds, feats, protos)
    return list(out[:CHUNKS]), list(out[CHUNKS:])


def merge_kernel(a, b, out):
    chans = a.shape[0] - STATS
    at, bt = a[chans : chans + 1, :], b[chans : chans + 1, :]
    top = jnp.maximum(at, bt)
    fa, fb = jnp.exp(at - top), jnp.exp(bt - top)
    out[:chans, :] = a[:chans, :] * fa + b[:chans, :] * fb
    out[chans : chans + 1, :] = top
    out[chans + 1 : chans + 2, :] = (
        a[chans + 1 : chans + 2, :] * fa + b[chans + 1 : chans + 2, :] * fb
    )
    out[chans + 2 :, :] = jnp.zeros((STATS - 2, a.shape[1]), F32)


def merge(a, b):
    return pl.pallas_call(
        merge_kernel,
        out_shape=jax.ShapeDtypeStruct(a.shape, F32),
        in_specs=[VMEM, VMEM],
        out_specs=VMEM,
        compiler_params=params(2),
        cost_estimate=cost(3 * a.size, 12 * a.size),
        name="merge",
    )(a, b)


def field_kernel(meta, seeds, *rest, sides):
    keep, got, near, far = rest[:CHUNKS], rest[CHUNKS : 2 * CHUNKS], *rest[2 * CHUNKS :][:2]
    rest = rest[2 * CHUNKS + 2 :]
    strips = rest[:sides]
    (
        taps, feats, refined, out,
        base, belief, second, lhs, lhs2, sums, result, out_sem,
    ) = rest[sides:]
    height, cols, chans = feats.shape
    count = sums.shape[1]
    classes = count // 4
    wide = cols + LANES
    sub, odd = meta[1], meta[2]
    half = count // 2
    first = pl.multiple_of(sub * half, half)
    other = pl.multiple_of((1 - sub) * half, half)
    part = chans // CHUNKS
    for refs, lanes in ((keep, pl.ds(first, half)), (got, pl.ds(other, half))):
        for i, ref in enumerate(refs):
            sums[i * part : (i + 1) * part, lanes] = ref[:part, :]
        sums[chans:, lanes] = ref[part:, :]
    pooled = sums[:chans, :] / sums[chans + 1 : chans + 2, :]
    length = jnp.sqrt(jnp.sum(pooled * pooled, axis=0, keepdims=True) + 1e-06)
    ready = (pooled / length).T
    for m in range(4):
        refined[:, m, :] = ready[m * classes : (m + 1) * classes, :]
    lead = (ready.astype(BF16).astype(F32) * SCALE).astype(BF16)

    labels = lax.broadcasted_iota(jnp.int32, (classes, 1), 0) + 1
    bonus = math.exp(SEED_REWARD)

    def share(grown):
        norm = jnp.sum(grown, axis=0, keepdims=True)
        return grown * (1.0 / jnp.maximum(norm, 1e-30))

    def unary(tokens, code):
        raw = lax.dot_general(lead, tokens, (((1,), (1,)), ((), ())), preferred_element_type=F32)
        parts = [raw[m * classes : (m + 1) * classes] for m in range(4)]
        top = functools.reduce(jnp.maximum, parts)
        top = jnp.max(top, axis=0, keepdims=True)
        top = jnp.where(code == 0, 1e30, top)
        grown = functools.reduce(jnp.add, [jnp.exp(part - top) for part in parts])
        grown = jnp.where(labels == code, grown * bonus, grown)
        return grown, share(grown)

    near_at = jnp.where(sub == 0, HALO + height, 0)
    far_at = jnp.where(sub == 0, 0, HALO + height)
    for i in range(HALO):
        for ref, at in ((near, near_at), (far, far_at)):
            tokens = ref[i * cols : (i + 1) * cols, :].astype(BF16)
            code = ref[HALO * cols + i : HALO * cols + i + 1, :].astype(jnp.int32)
            grown, early = unary(tokens, code)
            base[at + i, :, :cols] = grown
            belief[at + i, :, :cols] = early

    per = LANES // SIDE
    deep = height + 2 * HALO
    lane = lax.broadcasted_iota(jnp.int32, (classes, LANES), 1)
    for g in range(-(-deep // per)):
        found = []
        for strip in strips:
            tokens = strip[g * LANES : (g + 1) * LANES, :].astype(BF16)
            at = strip.shape[0] - STATS + g
            found.append(unary(tokens, strip[at : at + 1, :LANES].astype(jnp.int32)))
        for r in range(min(per, deep - g * per)):
            row = g * per + r
            for ref, one in ((base, 0), (belief, 1)):
                turn = (LANES + EDGE - r * SIDE) % LANES
                value = pltpu.roll(found[0][one], turn, 1) if turn else found[0][one]
                if len(found) > 1:
                    turn = (turn + SIDE) % LANES
                    more = pltpu.roll(found[1][one], turn, 1) if turn else found[1][one]
                    value = jnp.where(lane < EDGE + SIDE, value, more)
                ref[row, :, cols:] = value

    rows = 8

    @pl.loop(0, height // rows)
    def _(i):
        marks = jnp.where(meta[0] > 0, seeds[pl.ds(pl.multiple_of(i * rows, rows), rows), :] + 1, 0)
        for j in range(rows):
            row = i * rows + j
            grown, early = unary(feats[row], marks[j : j + 1, :])
            base[HALO + row, :, :cols] = grown
            belief[HALO + row, :, :cols] = early

    def mix(source, start, batch, into):
        for k in range(0, classes, 16):
            for c in range(0, cols + LANES, LANES):
                cells = [
                    source[start - REACH + j, k : k + 16, c : c + LANES]
                    for j in range(batch + 2 * REACH)
                ]
                for j in range(batch):
                    tall = TAPS[0] * cells[j + REACH]
                    for d in range(1, REACH + 1):
                        tall = tall + TAPS[d] * (cells[j + REACH - d] + cells[j + REACH + d])
                    high = tall.astype(BF16)
                    low = (tall - high.astype(F32)).astype(BF16)
                    at = slice(j * classes + k, j * classes + k + 16)
                    packed = 2 * cols
                    if c < cols:
                        into[at, c : c + LANES] = high
                        into[at, cols + c : cols + c + LANES] = low
                        keep = slice(0, 0)
                        if c == 0:
                            keep = slice(0, EDGE)
                        if c + LANES == cols:
                            keep = slice(LANES - EDGE, LANES)
                    else:
                        keep = slice(EDGE, LANES - EDGE)
                    if keep.stop:
                        for piece, place in ((high, packed), (low, packed + LANES)):
                            into[at, place + keep.start : place + keep.stop] = piece[:, keep]

    def sweep(source, start, stop, batch, settle):
        slots = (lhs, lhs2)

        @pl.loop(0, (stop - start) // (2 * batch))
        def _(i):
            for part, slot in enumerate(slots):
                mix(source, start + (2 * i + part) * batch, batch, slot)
            for part, slot in enumerate(slots):
                settle(2 * i + part, slot)

    def spread(slot, batch, rows, lanes):
        return jnp.dot(
            slot[: batch * classes, rows], taps[odd, rows, lanes], preferred_element_type=F32
        )

    def first(i, slot):
        main = spread(slot, 7, slice(0, 2 * wide), slice(0, cols))
        side = spread(slot, 7, slice(2 * cols, 2 * wide), slice(cols, wide))
        for j in range(7):
            row = REACH + i * 7 + j
            at = slice(j * classes, (j + 1) * classes)
            for got, lanes in ((main, slice(0, cols)), (side, slice(cols, wide))):
                sent = got[at, :] - belief[row, :, lanes]
                second[row, :, lanes] = share(base[row, :, lanes] * jnp.exp(sent))

    sweep(belief, REACH, height + HALO + REACH, 7, first)

    def leave(i):
        at = pl.ds(pl.multiple_of(i * 8, 8), 8)
        return pltpu.make_async_copy(result.at[:, at, :], out.at[:, at, :], out_sem.at[i])

    def last(i, slot):
        main = spread(slot, 8, slice(0, 2 * wide), slice(0, cols))
        for c in range(0, cols, LANES):
            lanes = slice(c, c + LANES)
            done = []
            for j in range(8):
                row = HALO + i * 8 + j
                sent = main[j * classes : (j + 1) * classes, lanes] - second[row, :, lanes]
                done.append(share(base[row, :, lanes] * jnp.exp(sent)))
            turned = jnp.transpose(jnp.stack(done), (1, 0, 2))
            result[:, pl.ds(pl.multiple_of(i * 8, 8), 8), lanes] = turned
        leave(i).start()

    sweep(second, HALO, HALO + height, 8, last)

    @pl.loop(0, height // 8)
    def _(i):
        leave(i).wait()


def field(meta, seeds, keep, got, near, far, strips, feats, count):
    height, cols, chans = feats.shape
    classes = count // 4
    wide = cols + LANES
    deep = height + 2 * HALO
    plane = pltpu.VMEM((deep, classes, wide), F32)
    return pl.pallas_call(
        functools.partial(field_kernel, sides=len(strips)),
        out_shape=(
            jax.ShapeDtypeStruct((classes, count // classes, chans), F32),
            jax.ShapeDtypeStruct((classes, height, cols), F32),
        ),
        in_specs=[SMEM] + [VMEM] * (5 + 2 * CHUNKS + len(strips)),
        out_specs=(VMEM, ANY),
        scratch_shapes=[
            plane,
            plane,
            plane,
            pltpu.VMEM((8 * classes, 2 * wide), BF16),
            pltpu.VMEM((8 * classes, 2 * wide), BF16),
            pltpu.VMEM((chans + STATS, count), F32),
            pltpu.VMEM((classes, height, cols), F32),
            pltpu.SemaphoreType.DMA((height // 8,)),
        ],
        compiler_params=params(38),
        cost_estimate=cost(8 * height * cols * chans * count, 16 << 20),
        name="field",
    )(meta, seeds, *keep, *got, near, far, *strips, jnp.asarray(across_taps(cols, len(strips)), BF16), feats)


def swap(x, axes, pairs):
    return lax.ppermute(x, axes, [p for a, b in pairs for p in ((a, b), (b, a))])


def on_device(features, seeds, valid_tiles, prototypes):
    height, cols, chans = features.shape
    classes, modes, _ = prototypes.shape
    count = classes * modes
    n_row, n_col = lax.axis_size("row"), lax.axis_size("col")
    sub, odd = lax.axis_index("sub"), lax.axis_index("col") % 2
    meta = jnp.stack([valid_tiles[0, 0], sub, odd]).astype(jnp.int32)

    near, far = ends(meta, seeds, features)
    far = swap(far, ("row", "sub"), [(2 * i + 1, 2 * i + 2) for i in range(n_row - 1)])
    near = swap(near, "sub", [(0, 1)])

    keep, give = pool(meta, seeds, features, prototypes)
    keep = [merge(k, swap(g, "sub", [(0, 1)])) for k, g in zip(keep, give)]

    near, far, _ = lax.optimization_barrier((near, far, keep))
    messages = [side(meta, seeds, near, far, features)]
    if n_col > 2:
        other = jnp.stack([meta[0], meta[1], 1 - odd])
        messages.append(side(other, seeds, near, far, features))

    def doubled(keep, axis, size, beside=()):
        stride = 1
        while stride < size:
            pairs = [(i, i | stride) for i in range(size) if not i & stride]
            got = [swap(k, axis, pairs) for k in keep]
            got, beside = lax.optimization_barrier((got, beside))
            keep = [merge(k, g) for k, g in zip(keep, got)]
            stride *= 2
        return keep, beside

    keep, messages = doubled(keep, "col", n_col, messages)
    messages, _ = lax.optimization_barrier((messages, keep))
    strips = [
        swap(message, "col", [(i, i + 1) for i in range(at, n_col - 1, 2)])
        for at, message in enumerate(messages)
    ]
    keep, _ = doubled(keep, "row", n_row)
    got = [swap(k, "sub", [(0, 1)]) for k in keep]
    refined, belief = field(meta, seeds, keep, got, near, far, strips, features, count)
    return refined, belief


def solution(mesh):
    placed = (
        P(("groups", "row", "sub"), "col", None),
        P(("groups", "row", "sub"), "col"),
        P(("groups", "row"), "col"),
        P("groups", None, None),
    )
    return jax.shard_map(
        on_device,
        mesh=mesh,
        in_specs=placed,
        out_specs=(P("groups", None, None), P("groups", ("row", "sub"), "col")),
        check_vma=False,
    )
```

time: 77.4 us -> 70.6 us (0.912)
  local copies, waits for them, and re-layouts: 5.03 us -> 1.01 us
  Pallas kernels: 41 us -> 39.9 us
  other arithmetic: 1.14 us -> 0.08 us
    pallas_call x1, Pallas kernels: 15.7 us -> 11.6 us  [pool(): pl.pallas_call(functools.partial(pool_kernel, rows=rows), out_shape=(piec...]
    unnamed x10 -> x8, local copies, waits for them, and re-layouts: 4.24 us -> 1.01 us
    pallas_call x1, Pallas kernels: 23.4 us -> 25.1 us  [field(): pl.pallas_call(functools.partial(field_kernel, sides=len(strips)), out_sh...]
    pallas_call x1, Pallas kernels: 0.88 us -> 2.38 us  [ends(): pl.pallas_call(ends_kernel, out_shape=(message, message), in_specs=[SMEM,...]
    transpose x1 -> x0, other arithmetic: 1.07 us -> none  [on_device(): protos = protos.transpose(1, 0, 2).reshape(count, chans)]
    reshape x1 -> x0, local copies, waits for them, and re-layouts: 0.78 us -> none  [on_device(): return (refined.reshape(classes, modes, chans), belief)]
  transfers between devices with their start and end apart: 8 -> 8, of which waited for: 6 -> 6; matrix products, arithmetic and copies ran while one was open for 1% -> 0% of each run, Pallas kernels for 21% -> 18%
where the time goes in v2:
time: 70.6 us; the launch traced here: 70.4 us
  Pallas kernels  39.9 us (57%)
  waiting for transfers between devices  15.3 us (22%)
  starting transfers between devices  12.7 us (18%)
  between operations  1.37 us (2%)
  local copies, waits for them, and re-layouts  1.01 us (1%)
    pallas_call x1, Pallas kernels, field(): pl.pallas_call(functools.partial(field_kernel, sides=len(strips)), out_sh...  25.1 us
    ppermute x8, waiting for transfers between devices, swap(): lax.ppermute(x, axes, [p for a, b in pairs for p in ((a, b), (b, a))])  15.3 us
    ppermute x8, starting transfers between devices, swap(): lax.ppermute(x, axes, [p for a, b in pairs for p in ((a, b), (b, a))])  12.7 us
    pallas_call x1, Pallas kernels, pool(): pl.pallas_call(functools.partial(pool_kernel, rows=rows), out_shape=(piec...  11.6 us
    pallas_call x1, Pallas kernels, ends(): pl.pallas_call(ends_kernel, out_shape=(message, message), in_specs=[SMEM,...  2.38 us
  transfers between devices with their start and end apart: 8, of which 6 were waited for; matrix products, arithmetic and copies ran while one was open for 0% of the time, Pallas kernels for 18%

profile of v2, /device:TPU:0, one launch (start us, length us, event | category | flops | bytes accessed | tf_op | source)
XLA Modules:
  0.0 70.4 jit_solution(4550479190525550984)
XLA Ops:
  1.3 0.1 pad_add_fusion.meta
  1.4 2.4 %ends.1 = (f32[1542,256]{1,0:T(8,128)S(1)}, f32[1542,256]{1,0:T(8,128)S(1)}) custom-call(s32[3]{0:T(128)S(1)} %pad_add_fusion.meta, s32[64,256]{1,0:T(8,128)} %seeds.7, bf16[64,256,256]{2,1,0:T(8,128)(2,1)} %rest_6_.1), custom_call_target="tpu_custom_call" | custom-call | bytes 4194304 | tf_op jit(solution)/shard_map/ends/pallas_call | solution.py:110
  3.8 0.5 collective-permute-start.2
  4.3 0.9 %collective-permute-start.3 = (f32[1542,256]{1,0:T(8,128)S(1)}, f32[1542,256]{1,0:T(8,128)S(1)}, u32[]{:S(2)}, u32[]{:S(2)}) collective-permute-start(f32[1542,256]{1,0:T(8,128)S(1)} %get-tuple-element.14), channel_id=1, source_target_pairs={{1,4},{4,1},{5,8},{8,5},{9,12},{12,9},{3,6},{6,3},{7,10},{10,7},{1... | collective-permute-start | bytes 4737032 | tf_op jit(solution)/shard_map/ppermute | solution.py:534
  5.2 0.1 copy-done
  5.3 0.9 %copy-done.2 = bf16[64,4,256]{2,1,0:T(4,128)(2,1)S(1)} copy-done((bf16[64,4,256]{2,1,0:T(4,128)(2,1)S(1)}, bf16[64,4,256]{2,1,0:T(4,128)(2,1)}, u32[]{:S(2)}) %copy-start.2) | copy-done | bytes 131096
  6.2 11.6 %pool.1 = (f32[264,128]{1,0:T(8,128)S(1)}, f32[264,128]{1,0:T(8,128)S(1)}) custom-call(s32[3]{0:T(128)S(1)} %pad_add_fusion.meta, s32[64,256]{1,0:T(8,128)S(1)} %copy-done.1, bf16[64,256,256]{2,1,0:T(8,128)(2,1)S(1)} %copy-done, bf16[64,4,256]{2,1,0:T(4,128)(2,1)S(1)} %copy-done.2), custom_call_target="tpu_custom_call" | custom-call | flops 4294967296 | bytes 8388608 | tf_op jit(solution)/shard_map/pool/pallas_call | solution.py:296
  17.8 3.9 %collective-permute-start = (f32[264,128]{1,0:T(8,128)S(1)}, f32[264,128]{1,0:T(8,128)S(1)}, u32[]{:S(2)}, u32[]{:S(2)}) collective-permute-start(f32[264,128]{1,0:T(8,128)S(1)} %get-tuple-element.12), channel_id=1, source_target_pairs={{0,1},{1,0},{2,3},{3,2},{4,5},{5,4},{6,7},{7,6},{8,9},{9,8},{10,11... | collective-permute-start | bytes 405512 | tf_op jit(solution)/shard_map/ppermute | solution.py:534
  21.6 1.0 %collective-permute-done.b = f32[264,128]{1,0:T(8,128)S(1)} collective-permute-done((f32[264,128]{1,0:T(8,128)S(1)}, f32[264,128]{1,0:T(8,128)S(1)}, u32[]{:S(2)}, u32[]{:S(2)}) %collective-permute-start) | collective-permute-done | bytes 135200 | tf_op jit(solution)/shard_map/ppermute | solution.py:534
  22.7 0.0 copy-start.3
  22.7 1.6 %collective-permute-start.1 = (f32[264,128]{1,0:T(8,128)S(1)}, f32[264,128]{1,0:T(8,128)S(1)}, u32[]{:S(2)}, u32[]{:S(2)}) collective-permute-start(f32[264,128]{1,0:T(8,128)S(1)} %merge.4.a), channel_id=1, source_target_pairs={{0,2},{2,0},{1,3},{3,1},{4,6},{6,4},{5,7},{7,5},{8,10},{10,8},{9,1... | collective-permute-start | bytes 405512 | tf_op jit(solution)/shard_map/ppermute | solution.py:534
  24.2 0.0 collective-permute-done.2.near.rest_2_
  24.2 0.0 collective-permute-done.3.far.rest_3_
  24.3 0.8 %side.1 = f32[648,256]{1,0:T(8,128)S(1)} custom-call(s32[3]{0:T(128)S(1)} %pad_add_fusion.meta, s32[64,256]{1,0:T(8,128)S(1)} %copy-done.1, f32[1542,256]{1,0:T(8,128)S(1)} %collective-permute-done.2.near.rest_2_, f32[1542,256]{1,0:T(8,128)S(1)} %collective-permute-done.3.far.rest_3_, bf16[64,256,256]{2,1,0:T(8,128)(2,1)S(1)} %copy-done), custom_call_target="tpu_custom_call" | custom-call | bytes 2097152 | tf_op jit(solution)/shard_map/side/pallas_call | solution.py:184
  25.0 3.6 %collective-permute-done.1.b = f32[264,128]{1,0:T(8,128)S(1)} collective-permute-done((f32[264,128]{1,0:T(8,128)S(1)}, f32[264,128]{1,0:T(8,128)S(1)}, u32[]{:S(2)}, u32[]{:S(2)}) %collective-permute-start.1) | collective-permute-done | bytes 135200 | tf_op jit(solution)/shard_map/ppermute | solution.py:534
  28.6 1.6 %collective-permute-start.7 = (f32[648,256]{1,0:T(8,128)S(1)}, f32[648,256]{1,0:T(8,128)S(1)}, u32[]{:S(2)}, u32[]{:S(2)}) collective-permute-start(f32[648,256]{1,0:T(8,128)S(1)} %side.1), channel_id=1, source_target_pairs={{0,2},{2,0},{1,3},{3,1},{4,6},{6,4},{5,7},{7,5},{8,10},{10,8},{9,1... | collective-permute-start | bytes 1990664 | tf_op jit(solution)/shard_map/ppermute | solution.py:534
  30.2 1.6 %collective-permute-start.4 = (f32[264,128]{1,0:T(8,128)S(1)}, f32[264,128]{1,0:T(8,128)S(1)}, u32[]{:S(2)}, u32[]{:S(2)}) collective-permute-start(f32[264,128]{1,0:T(8,128)S(1)} %merge.5.a), channel_id=1, source_target_pairs={{0,4},{4,0},{8,12},{12,8},{1,5},{5,1},{9,13},{13,9},{2,6},{6,2},{1... | collective-permute-start | bytes 405512 | tf_op jit(solution)/shard_map/ppermute | solution.py:534
  31.8 3.7 %collective-permute-done.4.b = f32[264,128]{1,0:T(8,128)S(1)} collective-permute-done((f32[264,128]{1,0:T(8,128)S(1)}, f32[264,128]{1,0:T(8,128)S(1)}, u32[]{:S(2)}, u32[]{:S(2)}) %collective-permute-start.4) | collective-permute-done | bytes 135200 | tf_op jit(solution)/shard_map/ppermute | solution.py:534
  35.5 2.7 %collective-permute-start.5 = (f32[264,128]{1,0:T(8,128)S(1)}, f32[264,128]{1,0:T(8,128)S(1)}, u32[]{:S(2)}, u32[]{:S(2)}) collective-permute-start(f32[264,128]{1,0:T(8,128)S(1)} %merge.6.a), channel_id=1, source_target_pairs={{0,8},{8,0},{4,12},{12,4},{1,9},{9,1},{5,13},{13,5},{2,10},{10,2},... | collective-permute-start | bytes 405512 | tf_op jit(solution)/shard_map/ppermute | solution.py:534
  38.1 5.6 %collective-permute-done.5.b = f32[264,128]{1,0:T(8,128)S(1)} collective-permute-done((f32[264,128]{1,0:T(8,128)S(1)}, f32[264,128]{1,0:T(8,128)S(1)}, u32[]{:S(2)}, u32[]{:S(2)}) %collective-permute-start.5) | collective-permute-done | bytes 135200 | tf_op jit(solution)/shard_map/ppermute | solution.py:534
  43.8 0.1 collective-permute-start.6
  43.9 1.3 %collective-permute-done.6.rest_1_ = f32[264,128]{1,0:T(8,128)S(1)} collective-permute-done((f32[264,128]{1,0:T(8,128)S(1)}, f32[264,128]{1,0:T(8,128)S(1)}, u32[]{:S(2)}, u32[]{:S(2)}) %collective-permute-start.6) | collective-permute-done | bytes 135200 | tf_op jit(solution)/shard_map/ppermute | solution.py:534
  45.2 0.1 collective-permute-done.7.rest_4_
  45.3 25.1 %field.1 = (f32[64,4,256]{2,1,0:T(4,128)}, f32[64,64,256]{2,1,0:T(8,128)}) custom-call(s32[3]{0:T(128)S(1)} %pad_add_fusion.meta, s32[64,256]{1,0:T(8,128)S(1)} %copy-done.1, f32[264,128]{1,0:T(8,128)S(1)} %merge.7.rest_0_, f32[264,128]{1,0:T(8,128)S(1)} %collective-permute-done.6.rest_1_, f32[1542,256]{1,0:T(8,128)S(1)} %collective-permute-done.2.near.rest_2_, ...), custom_call_target="tpu_custom_call" | custom-call | flops 8589934592 | bytes 16777216 | tf_op jit(solution)/shard_map/field/pallas_call | solution.py:509
  (9 shorter events, 0.1 us)
Async XLA Ops:
  1.4 3.9 %copy-start = (bf16[64,256,256]{2,1,0:T(8,128)(2,1)S(1)}, bf16[64,256,256]{2,1,0:T(8,128)(2,1)}, u32[]{:S(2)}) copy-start(bf16[64,256,256]{2,1,0:T(8,128)(2,1)} %rest_6_.1) | copy-start | bytes 25165828
  1.4 3.9 %copy-start.1 = (s32[64,256]{1,0:T(8,128)S(1)}, s32[64,256]{1,0:T(8,128)}, u32[]{:S(2)}) copy-start(s32[64,256]{1,0:T(8,128)} %seeds.7) | copy-start | bytes 196612
  3.8 20.5 %collective-permute-start.2 = (f32[1542,256]{1,0:T(8,128)S(1)}, f32[1542,256]{1,0:T(8,128)S(1)}, u32[]{:S(2)}, u32[]{:S(2)}) collective-permute-start(f32[1542,256]{1,0:T(8,128)S(1)} %get-tuple-element.13), channel_id=1, source_target_pairs={{0,1},{1,0},{2,3},{3,2},{4,5},{5,4},{6,7},{7,6},{8,9},{9,8},{10,11... | collective-permute-start | bytes 4737032 | tf_op jit(solution)/shard_map/ppermute | solution.py:534
  4.3 20.0 %collective-permute-start.3 = (f32[1542,256]{1,0:T(8,128)S(1)}, f32[1542,256]{1,0:T(8,128)S(1)}, u32[]{:S(2)}, u32[]{:S(2)}) collective-permute-start(f32[1542,256]{1,0:T(8,128)S(1)} %get-tuple-element.14), channel_id=1, source_target_pairs={{1,4},{4,1},{5,8},{8,5},{9,12},{12,9},{3,6},{6,3},{7,10},{10,7},{1... | collective-permute-start | bytes 4737032 | tf_op jit(solution)/shard_map/ppermute | solution.py:534
  5.3 0.9 %copy-start.2 = (bf16[64,4,256]{2,1,0:T(4,128)(2,1)S(1)}, bf16[64,4,256]{2,1,0:T(4,128)(2,1)}, u32[]{:S(2)}) copy-start(bf16[64,4,256]{2,1,0:T(4,128)(2,1)} %given.1) | copy-start | bytes 393220
  17.8 4.9 %collective-permute-start = (f32[264,128]{1,0:T(8,128)S(1)}, f32[264,128]{1,0:T(8,128)S(1)}, u32[]{:S(2)}, u32[]{:S(2)}) collective-permute-start(f32[264,128]{1,0:T(8,128)S(1)} %get-tuple-element.12), channel_id=1, source_target_pairs={{0,1},{1,0},{2,3},{3,2},{4,5},{5,4},{6,7},{7,6},{8,9},{9,8},{10,11... | collective-permute-start | bytes 405512 | tf_op jit(solution)/shard_map/ppermute | solution.py:534
  22.7 22.7 %copy-start.3 = (bf16[2,768,384]{2,1,0:T(8,128)(2,1)S(1)}, bf16[2,768,384]{2,1,0:T(8,128)(2,1)}, u32[]{:S(2)}) copy-start(bf16[2,768,384]{2,1,0:T(8,128)(2,1)} %constant.21.clone.rest_5_) | copy-start | bytes 3538948
  22.7 5.9 %collective-permute-start.1 = (f32[264,128]{1,0:T(8,128)S(1)}, f32[264,128]{1,0:T(8,128)S(1)}, u32[]{:S(2)}, u32[]{:S(2)}) collective-permute-start(f32[264,128]{1,0:T(8,128)S(1)} %merge.4.a), channel_id=1, source_target_pairs={{0,2},{2,0},{1,3},{3,1},{4,6},{6,4},{5,7},{7,5},{8,10},{10,8},{9,1... | collective-permute-start | bytes 405512 | tf_op jit(solution)/shard_map/ppermute | solution.py:534
  28.6 16.7 %collective-permute-start.7 = (f32[648,256]{1,0:T(8,128)S(1)}, f32[648,256]{1,0:T(8,128)S(1)}, u32[]{:S(2)}, u32[]{:S(2)}) collective-permute-start(f32[648,256]{1,0:T(8,128)S(1)} %side.1), channel_id=1, source_target_pairs={{0,2},{2,0},{1,3},{3,1},{4,6},{6,4},{5,7},{7,5},{8,10},{10,8},{9,1... | collective-permute-start | bytes 1990664 | tf_op jit(solution)/shard_map/ppermute | solution.py:534
  30.2 5.3 %collective-permute-start.4 = (f32[264,128]{1,0:T(8,128)S(1)}, f32[264,128]{1,0:T(8,128)S(1)}, u32[]{:S(2)}, u32[]{:S(2)}) collective-permute-start(f32[264,128]{1,0:T(8,128)S(1)} %merge.5.a), channel_id=1, source_target_pairs={{0,4},{4,0},{8,12},{12,8},{1,5},{5,1},{9,13},{13,9},{2,6},{6,2},{1... | collective-permute-start | bytes 405512 | tf_op jit(solution)/shard_map/ppermute | solution.py:534
  35.5 8.2 %collective-permute-start.5 = (f32[264,128]{1,0:T(8,128)S(1)}, f32[264,128]{1,0:T(8,128)S(1)}, u32[]{:S(2)}, u32[]{:S(2)}) collective-permute-start(f32[264,128]{1,0:T(8,128)S(1)} %merge.6.a), channel_id=1, source_target_pairs={{0,8},{8,0},{4,12},{12,4},{1,9},{9,1},{5,13},{13,5},{2,10},{10,2},... | collective-permute-start | bytes 405512 | tf_op jit(solution)/shard_map/ppermute | solution.py:534
  43.8 1.4 %collective-permute-start.6 = (f32[264,128]{1,0:T(8,128)S(1)}, f32[264,128]{1,0:T(8,128)S(1)}, u32[]{:S(2)}, u32[]{:S(2)}) collective-permute-start(f32[264,128]{1,0:T(8,128)S(1)} %merge.7.rest_0_), channel_id=1, source_target_pairs={{0,1},{1,0},{2,3},{3,2},{4,5},{5,4},{6,7},{7,6},{8,9},{9,8},{10,11... | collective-permute-start | bytes 405512 | tf_op jit(solution)/shard_map/ppermute | solution.py:534

commit v3 on v2

--- a/solution.py
+++ b/solution.py
@@ -17,11 +17,12 @@
 HALO = ITERS * REACH
 LANES = 128
 STATS = 8
-SIDE = 8
+SIDE = 6
+PER = LANES // SIDE
 EDGE = 32
 CHUNKS = 1
 GAIN = 1.461325
-TAPS = [math.exp(-(d * d) / 8.0) / GAIN for d in range(REACH + 1)]
+TAPS = [math.exp(-(d * d) / 8.0) for d in range(REACH + 1)]
 F32 = jnp.float32
 BF16 = jnp.bfloat16
 VMEM = pl.BlockSpec(memory_space=pltpu.VMEM)
@@ -72,8 +73,11 @@
     return np.stack(both)
 
 
-def ends_kernel(meta, seeds, feats, near, far, held, labels, sem):
-    height, cols, chans = feats.shape
+def ends_kernel(meta, seeds, feats, given, near, far, protos, held, labels, raw, sem):
+    height, cols, chans = feats.shape
+    classes, modes, _ = given.shape
+    order = pltpu.make_async_copy(given, raw, sem.at[4])
+    order.start()
     fetch = [
         pltpu.make_async_copy(feats.at[pl.ds(at, HALO)], held.at[i], sem.at[i])
         for i, at in enumerate((0, height - HALO))
@@ -83,6 +87,10 @@
     ]
     for copy in fetch:
         copy.start()
+    order.wait()
+    doubled = raw[...].astype(F32) * SCALE
+    for m in range(modes):
+        protos[m * classes : (m + 1) * classes, :] = doubled[:, m, :].astype(BF16)
     for copy in fetch:
         copy.wait()
 
@@ -104,86 +112,96 @@
         write(far, 1)
 
 
-def ends(meta, seeds, feats):
-    height, cols, chans = feats.shape
+def ends(meta, seeds, feats, given):
+    height, cols, chans = feats.shape
+    classes, modes, _ = given.shape
     message = jax.ShapeDtypeStruct((HALO * cols + HALO, chans), F32)
     return pl.pallas_call(
         ends_kernel,
-        out_shape=(message, message),
-        in_specs=[SMEM, HBM, HBM],
-        out_specs=(VMEM, VMEM),
+        out_shape=(message, message, jax.ShapeDtypeStruct((classes * modes, chans), BF16)),
+        in_specs=[SMEM, HBM, HBM, HBM],
+        out_specs=(VMEM, VMEM, VMEM),
         scratch_shapes=[
             pltpu.VMEM((2, HALO, cols, chans), BF16),
             pltpu.VMEM((2, 8, cols), jnp.int32),
-            pltpu.SemaphoreType.DMA((4,)),
+            pltpu.VMEM(given.shape, BF16),
+            pltpu.SemaphoreType.DMA((5,)),
         ],
         compiler_params=params(8),
         cost_estimate=cost(0, 4 << 20),
         name="ends",
-    )(meta, in_hbm(seeds), in_hbm(feats))
+    )(meta, in_hbm(seeds), in_hbm(feats), in_hbm(given))
 
 
 def side_kernel(meta, seeds, near, far, feats, out, marks):
     height, cols, chans = feats.shape
     deep = marks.shape[0]
-    width = 2 * SIDE
+    width = 16
     sub, left = meta[1], meta[2]
     marks[...] = jnp.zeros_like(marks)
     marks[HALO : HALO + height, :] = jnp.where(meta[0] > 0, seeds[...] + 1, 0).astype(F32)
     low, skip = HALO + height, jnp.where(left > 0, 0, cols - SIDE)
-    skip = pl.multiple_of(skip, SIDE)
-
-    def ends_of(ref, at):
+
+    def place(row):
+        at = row // PER * LANES + row % PER * SIDE
+        return slice(at, at + SIDE)
+
+    def ends_of(ref, at, last):
         marks[at : at + HALO, :] = ref[HALO * cols :, :]
         for r in range(HALO):
-            out[(at + r) * SIDE : (at + r + 1) * SIDE, :] = ref[pl.ds(r * cols + skip, SIDE), :]
-
-    @pl.when(sub == 0)
+            first = (r + 1) * cols - SIDE if last else r * cols
+            out[place(at + r), :] = ref[first : first + SIDE, :]
+
+    def fill(last):
+        @pl.when(sub == 0)
+        def _():
+            ends_of(near, low, last)
+            ends_of(far, 0, last)
+
+        @pl.when(sub != 0)
+        def _():
+            ends_of(far, low, last)
+            ends_of(near, 0, last)
+
+        for r in range(height):
+            if last:
+                rows = feats[r, cols - width :].astype(F32)[width - SIDE :]
+            else:
+                rows = feats[r, :width].astype(F32)[:SIDE]
+            out[place(HALO + r), :] = rows
+
+    groups = deep // PER
+    out[groups * LANES :, :] = jnp.zeros((STATS, chans), F32)
+    for g in range(groups):
+        bare = max(0, min(PER, height + 2 * HALO - g * PER)) * SIDE
+        out[g * LANES + bare : (g + 1) * LANES, :] = jnp.zeros((LANES - bare, chans), F32)
+
+    @pl.when(left > 0)
     def _():
-        ends_of(near, low)
-        ends_of(far, 0)
-
-    @pl.when(sub != 0)
+        fill(False)
+
+    @pl.when(left == 0)
     def _():
-        ends_of(far, low)
-        ends_of(near, 0)
+        fill(True)
 
     lane = lax.broadcasted_iota(jnp.int32, (cols, LANES), 1)
     source = lax.broadcasted_iota(jnp.int32, (cols, LANES), 0)
     spread = (source == lane % SIDE + skip).astype(BF16)
     spun = jnp.dot(marks[...].astype(BF16), spread, preferred_element_type=F32)
-    per = LANES // SIDE
-    groups = deep // per
-    mine = lax.broadcasted_iota(jnp.int32, (per, LANES), 1) // SIDE
-    mine = mine == lax.broadcasted_iota(jnp.int32, (per, LANES), 0)
-    out[deep * SIDE :, :] = jnp.zeros((STATS, chans), F32)
+    mine = lax.broadcasted_iota(jnp.int32, (PER, LANES), 1) // SIDE
+    mine = mine == lax.broadcasted_iota(jnp.int32, (PER, LANES), 0)
     for g in range(groups):
-        row = jnp.where(mine, spun[g * per : (g + 1) * per], 0.0)
-        out[deep * SIDE + g : deep * SIDE + g + 1, :LANES] = jnp.sum(row, axis=0, keepdims=True)
-    out[(height + 2 * HALO) * SIDE : deep * SIDE, :] = jnp.zeros(
-        ((deep - height - 2 * HALO) * SIDE, chans), F32
-    )
-
-    @pl.when(left > 0)
-    def _():
-        for r in range(height):
-            at = (HALO + r) * SIDE
-            out[at : at + SIDE, :] = feats[r, :width].astype(F32)[:SIDE]
-
-    @pl.when(left == 0)
-    def _():
-        for r in range(height):
-            at = (HALO + r) * SIDE
-            out[at : at + SIDE, :] = feats[r, cols - width :].astype(F32)[SIDE:]
+        row = jnp.where(mine, spun[g * PER : (g + 1) * PER], 0.0)
+        at = groups * LANES + g
+        out[at : at + 1, :LANES] = jnp.sum(row, axis=0, keepdims=True)
 
 
 def side(meta, seeds, near, far, feats):
     height, cols, chans = feats.shape
-    per = LANES // SIDE
-    deep = -(-(height + 2 * HALO) // per) * per
+    deep = -(-(height + 2 * HALO) // PER) * PER
     return pl.pallas_call(
         side_kernel,
-        out_shape=jax.ShapeDtypeStruct((deep * SIDE + STATS, chans), F32),
+        out_shape=jax.ShapeDtypeStruct((deep // PER * LANES + STATS, chans), F32),
         in_specs=[SMEM, VMEM, VMEM, VMEM, VMEM],
         out_specs=VMEM,
         scratch_shapes=[pltpu.VMEM((deep, cols), F32)],
@@ -193,16 +211,13 @@
     )(meta, seeds, near, far, feats)
 
 
-def pool_kernel(meta, seeds, feats, given, *rest, rows):
+def pool_kernel(meta, seeds, feats, protos, *rest, rows):
     keep, give, scratch = rest[:CHUNKS], rest[CHUNKS : 2 * CHUNKS], rest[2 * CHUNKS :]
     score, weight, top = scratch[:2], scratch[2:4], scratch[4:6]
-    acc, peak, total, protos = scratch[6:]
-    height, cols, chans = feats.shape
-    classes, modes, _ = given.shape
-    count = classes * modes
-    wide = given[...].astype(F32) * SCALE
-    for m in range(modes):
-        protos[m * classes : (m + 1) * classes, :] = wide[:, m, :].astype(BF16)
+    acc, peak, total = scratch[6:]
+    height, cols, chans = feats.shape
+    count = protos.shape[0]
+    classes = count // 4
     chunks = height // rows
     acc[...] = jnp.zeros_like(acc)
     total[...] = jnp.zeros_like(total)
@@ -288,8 +303,8 @@
 
 def pool(meta, seeds, feats, protos):
     height, cols, chans = feats.shape
-    count = protos.shape[0] * protos.shape[1]
-    rows = 4
+    count = protos.shape[0]
+    rows = 16
     piece = jax.ShapeDtypeStruct((chans // CHUNKS + STATS, count // 2), F32)
     flat = (count, rows * cols)
     narrow = pltpu.VMEM((count, LANES), F32)
@@ -301,8 +316,8 @@
         scratch_shapes=[pltpu.VMEM(flat, F32)] * 2
         + [pltpu.VMEM(flat, BF16)] * 2
         + [narrow] * 2
-        + [pltpu.VMEM((count, chans), F32), narrow, narrow, pltpu.VMEM((count, chans), BF16)],
-        compiler_params=params(8),
+        + [pltpu.VMEM((count, chans), F32), narrow, narrow],
+        compiler_params=params(24),
         cost_estimate=cost(4 * height * cols * chans * count, height * cols * chans * 2),
         name="pool",
     )(meta, seeds, feats, protos)
@@ -389,7 +404,7 @@
             base[at + i, :, :cols] = grown
             belief[at + i, :, :cols] = early
 
-    per = LANES // SIDE
+    per = PER
     deep = height + 2 * HALO
     lane = lax.broadcasted_iota(jnp.int32, (classes, LANES), 1)
     for g in range(-(-deep // per)):
@@ -409,7 +424,7 @@
                     value = jnp.where(lane < EDGE + SIDE, value, more)
                 ref[row, :, cols:] = value
 
-    rows = 8
+    rows = 16
 
     @pl.loop(0, height // rows)
     def _(i):
@@ -428,7 +443,7 @@
                     for j in range(batch + 2 * REACH)
                 ]
                 for j in range(batch):
-                    tall = TAPS[0] * cells[j + REACH]
+                    tall = cells[j + REACH]
                     for d in range(1, REACH + 1):
                         tall = tall + TAPS[d] * (cells[j + REACH - d] + cells[j + REACH + d])
                     high = tall.astype(BF16)
@@ -471,7 +486,7 @@
             row = REACH + i * 7 + j
             at = slice(j * classes, (j + 1) * classes)
             for got, lanes in ((main, slice(0, cols)), (side, slice(cols, wide))):
-                sent = got[at, :] - belief[row, :, lanes]
+                sent = got[at, :] * (1 / GAIN) - belief[row, :, lanes]
                 second[row, :, lanes] = share(base[row, :, lanes] * jnp.exp(sent))
 
     sweep(belief, REACH, height + HALO + REACH, 7, first)
@@ -487,7 +502,8 @@
             done = []
             for j in range(8):
                 row = HALO + i * 8 + j
-                sent = main[j * classes : (j + 1) * classes, lanes] - second[row, :, lanes]
+                own = main[j * classes : (j + 1) * classes, lanes]
+                sent = own * (1 / GAIN) - second[row, :, lanes]
                 done.append(share(base[row, :, lanes] * jnp.exp(sent)))
             turned = jnp.transpose(jnp.stack(done), (1, 0, 2))
             result[:, pl.ds(pl.multiple_of(i * 8, 8), 8), lanes] = turned
@@ -542,36 +558,35 @@
     sub, odd = lax.axis_index("sub"), lax.axis_index("col") % 2
     meta = jnp.stack([valid_tiles[0, 0], sub, odd]).astype(jnp.int32)
 
-    near, far = ends(meta, seeds, features)
+    near, far, protos = ends(meta, seeds, features, prototypes)
     far = swap(far, ("row", "sub"), [(2 * i + 1, 2 * i + 2) for i in range(n_row - 1)])
     near = swap(near, "sub", [(0, 1)])
 
-    keep, give = pool(meta, seeds, features, prototypes)
+    keep, give = pool(meta, seeds, features, protos)
     keep = [merge(k, swap(g, "sub", [(0, 1)])) for k, g in zip(keep, give)]
 
+    def doubled(keep, axis, size, beside=()):
+        stride = 1
+        while stride < size:
+            pairs = [(i, i | stride) for i in range(size) if not i & stride]
+            got = [swap(k, axis, pairs) for k in keep]
+            if stride == 1:
+                got, beside = lax.optimization_barrier((got, beside))
+            keep = [merge(k, g) for k, g in zip(keep, got)]
+            stride *= 2
+        return keep, beside
+
+    keep, _ = doubled(keep, "col", n_col)
     near, far, _ = lax.optimization_barrier((near, far, keep))
     messages = [side(meta, seeds, near, far, features)]
     if n_col > 2:
         other = jnp.stack([meta[0], meta[1], 1 - odd])
         messages.append(side(other, seeds, near, far, features))
-
-    def doubled(keep, axis, size, beside=()):
-        stride = 1
-        while stride < size:
-            pairs = [(i, i | stride) for i in range(size) if not i & stride]
-            got = [swap(k, axis, pairs) for k in keep]
-            got, beside = lax.optimization_barrier((got, beside))
-            keep = [merge(k, g) for k, g in zip(keep, got)]
-            stride *= 2
-        return keep, beside
-
-    keep, messages = doubled(keep, "col", n_col, messages)
-    messages, _ = lax.optimization_barrier((messages, keep))
+    keep, messages = doubled(keep, "row", n_row, messages)
     strips = [
         swap(message, "col", [(i, i + 1) for i in range(at, n_col - 1, 2)])
         for at, message in enumerate(messages)
     ]
-    keep, _ = doubled(keep, "row", n_row)
     got = [swap(k, "sub", [(0, 1)]) for k in keep]
     refined, belief = field(meta, seeds, keep, got, near, far, strips, features, count)
     return refined, belief

time: 70.6 us -> 68.3 us (0.967)
  Pallas kernels: 39.9 us -> 37.8 us
  local copies, waits for them, and re-layouts: 1.01 us -> 0.23 us
    pallas_call x1, Pallas kernels: 11.6 us -> 10.2 us  [pool(): pl.pallas_call(functools.partial(pool_kernel, rows=rows), out_shape=(piec...]
    pallas_call x1, Pallas kernels: 25.1 us -> 24.1 us  [field(): pl.pallas_call(functools.partial(field_kernel, sides=len(strips)), out_sh...]
    unnamed x8 -> x6, local copies, waits for them, and re-layouts: 1.01 us -> 0.23 us
  transfers between devices with their start and end apart: 8 -> 8, of which waited for: 6 -> 6; matrix products, arithmetic and copies ran while one was open for 0% -> 0% of each run, Pallas kernels for 18% -> 17%
where the time goes in v3:
time: 68.3 us; the launch traced here: 68.1 us
  Pallas kernels  37.8 us (55%)
  waiting for transfers between devices  15.9 us (23%)
  starting transfers between devices  12.6 us (18%)
  between operations  1.53 us (2%)
    pallas_call x1, Pallas kernels, field(): pl.pallas_call(functools.partial(field_kernel, sides=len(strips)), out_sh...  24.1 us
    ppermute x8, waiting for transfers between devices, swap(): lax.ppermute(x, axes, [p for a, b in pairs for p in ((a, b), (b, a))])  15.9 us
    ppermute x8, starting transfers between devices, swap(): lax.ppermute(x, axes, [p for a, b in pairs for p in ((a, b), (b, a))])  12.6 us
    pallas_call x1, Pallas kernels, pool(): pl.pallas_call(functools.partial(pool_kernel, rows=rows), out_shape=(piec...  10.2 us
    pallas_call x1, Pallas kernels, ends(): pl.pallas_call(ends_kernel, out_shape=(message, message, jax.ShapeDtypeSt...  2.45 us
  transfers between devices with their start and end apart: 8, of which 6 were waited for; matrix products, arithmetic and copies ran while one was open for 0% of the time, Pallas kernels for 17%

profile of v3, /device:TPU:0, one launch (start us, length us, event | category | flops | bytes accessed | tf_op | source)
XLA Modules:
  0.0 68.1 jit_solution(9278113194180338175)
XLA Ops:
  1.3 0.1 pad_add_fusion.meta
  1.4 2.5 %ends.1 = (f32[1542,256]{1,0:T(8,128)S(1)}, f32[1542,256]{1,0:T(8,128)S(1)}, bf16[256,256]{1,0:T(8,128)(2,1)S(1)}) custom-call(s32[3]{0:T(128)S(1)} %pad_add_fusion.meta, s32[64,256]{1,0:T(8,128)} %seeds.7, bf16[64,256,256]{2,1,0:T(8,128)(2,1)} %rest_6_.1, bf16[64,4,256]{2,1,0:T(4,128)(2,1)} %given.1), custom_call_target="tpu_custom_call" | custom-call | bytes 4194304 | tf_op jit(solution)/shard_map/ends/pallas_call | solution.py:119
  3.8 0.5 collective-permute-start.3
  4.3 0.8 %collective-permute-start.4 = (f32[1542,256]{1,0:T(8,128)S(1)}, f32[1542,256]{1,0:T(8,128)S(1)}, u32[]{:S(2)}, u32[]{:S(2)}) collective-permute-start(f32[1542,256]{1,0:T(8,128)S(1)} %get-tuple-element.15), channel_id=1, source_target_pairs={{1,4},{4,1},{5,8},{8,5},{9,12},{12,9},{3,6},{6,3},{7,10},{10,7},{1... | collective-permute-start | bytes 4737032 | tf_op jit(solution)/shard_map/ppermute | solution.py:550
  5.1 0.2 copy-done
  5.3 10.2 %pool.1 = (f32[264,128]{1,0:T(8,128)S(1)}, f32[264,128]{1,0:T(8,128)S(1)}) custom-call(s32[3]{0:T(128)S(1)} %pad_add_fusion.meta, s32[64,256]{1,0:T(8,128)S(1)} %copy-done.1, bf16[64,256,256]{2,1,0:T(8,128)(2,1)S(1)} %copy-done, bf16[256,256]{1,0:T(8,128)(2,1)S(1)} %get-tuple-element.11.protos), custom_call_target="tpu_custom_call" | custom-call | flops 4294967296 | bytes 8388608 | tf_op jit(solution)/shard_map/pool/pallas_call | solution.py:311
  15.5 3.9 %collective-permute-start = (f32[264,128]{1,0:T(8,128)S(1)}, f32[264,128]{1,0:T(8,128)S(1)}, u32[]{:S(2)}, u32[]{:S(2)}) collective-permute-start(f32[264,128]{1,0:T(8,128)S(1)} %get-tuple-element.13), channel_id=1, source_target_pairs={{0,1},{1,0},{2,3},{3,2},{4,5},{5,4},{6,7},{7,6},{8,9},{9,8},{10,11... | collective-permute-start | bytes 405512 | tf_op jit(solution)/shard_map/ppermute | solution.py:550
  19.4 1.0 %collective-permute-done.b = f32[264,128]{1,0:T(8,128)S(1)} collective-permute-done((f32[264,128]{1,0:T(8,128)S(1)}, f32[264,128]{1,0:T(8,128)S(1)}, u32[]{:S(2)}, u32[]{:S(2)}) %collective-permute-start) | collective-permute-done | bytes 135200 | tf_op jit(solution)/shard_map/ppermute | solution.py:550
  20.4 1.6 %collective-permute-start.1 = (f32[264,128]{1,0:T(8,128)S(1)}, f32[264,128]{1,0:T(8,128)S(1)}, u32[]{:S(2)}, u32[]{:S(2)}) collective-permute-start(f32[264,128]{1,0:T(8,128)S(1)} %merge.4.a), channel_id=1, source_target_pairs={{0,2},{2,0},{1,3},{3,1},{4,6},{6,4},{5,7},{7,5},{8,10},{10,8},{9,1... | collective-permute-start | bytes 405512 | tf_op jit(solution)/shard_map/ppermute | solution.py:550
  22.0 4.3 %collective-permute-done.1.b = f32[264,128]{1,0:T(8,128)S(1)} collective-permute-done((f32[264,128]{1,0:T(8,128)S(1)}, f32[264,128]{1,0:T(8,128)S(1)}, u32[]{:S(2)}, u32[]{:S(2)}) %collective-permute-start.1) | collective-permute-done | bytes 135200 | tf_op jit(solution)/shard_map/ppermute | solution.py:550
  26.4 0.0 copy-start.2
  26.4 1.6 %collective-permute-start.2 = (f32[264,128]{1,0:T(8,128)S(1)}, f32[264,128]{1,0:T(8,128)S(1)}, u32[]{:S(2)}, u32[]{:S(2)}) collective-permute-start(f32[264,128]{1,0:T(8,128)S(1)} %merge.5.a), channel_id=1, source_target_pairs={{0,4},{4,0},{8,12},{12,8},{1,5},{5,1},{9,13},{13,9},{2,6},{6,2},{1... | collective-permute-start | bytes 405512 | tf_op jit(solution)/shard_map/ppermute | solution.py:550
  28.0 0.0 collective-permute-done.3.near.rest_2_
  28.0 0.0 collective-permute-done.4.far.rest_3_
  28.0 1.0 %side.1 = f32[520,256]{1,0:T(8,128)S(1)} custom-call(s32[3]{0:T(128)S(1)} %pad_add_fusion.meta, s32[64,256]{1,0:T(8,128)S(1)} %copy-done.1, f32[1542,256]{1,0:T(8,128)S(1)} %collective-permute-done.3.near.rest_2_, f32[1542,256]{1,0:T(8,128)S(1)} %collective-permute-done.4.far.rest_3_, bf16[64,256,256]{2,1,0:T(8,128)(2,1)S(1)} %copy-done), custom_call_target="tpu_custom_call" | custom-call | bytes 2097152 | tf_op jit(solution)/shard_map/side/pallas_call | solution.py:202
  29.0 2.5 %collective-permute-done.2.b = f32[264,128]{1,0:T(8,128)S(1)} collective-permute-done((f32[264,128]{1,0:T(8,128)S(1)}, f32[264,128]{1,0:T(8,128)S(1)}, u32[]{:S(2)}, u32[]{:S(2)}) %collective-permute-start.2) | collective-permute-done | bytes 135200 | tf_op jit(solution)/shard_map/ppermute | solution.py:550
  31.5 1.5 %collective-permute-start.7 = (f32[520,256]{1,0:T(8,128)S(1)}, f32[520,256]{1,0:T(8,128)S(1)}, u32[]{:S(2)}, u32[]{:S(2)}) collective-permute-start(f32[520,256]{1,0:T(8,128)S(1)} %side.1), channel_id=1, source_target_pairs={{0,2},{2,0},{1,3},{3,1},{4,6},{6,4},{5,7},{7,5},{8,10},{10,8},{9,1... | collective-permute-start | bytes 1597448 | tf_op jit(solution)/shard_map/ppermute | solution.py:550
  33.0 2.7 %collective-permute-start.5 = (f32[264,128]{1,0:T(8,128)S(1)}, f32[264,128]{1,0:T(8,128)S(1)}, u32[]{:S(2)}, u32[]{:S(2)}) collective-permute-start(f32[264,128]{1,0:T(8,128)S(1)} %merge.6.a), channel_id=1, source_target_pairs={{0,8},{8,0},{4,12},{12,4},{1,9},{9,1},{5,13},{13,5},{2,10},{10,2},... | collective-permute-start | bytes 405512 | tf_op jit(solution)/shard_map/ppermute | solution.py:550
  35.6 4.8 %collective-permute-done.5.b = f32[264,128]{1,0:T(8,128)S(1)} collective-permute-done((f32[264,128]{1,0:T(8,128)S(1)}, f32[264,128]{1,0:T(8,128)S(1)}, u32[]{:S(2)}, u32[]{:S(2)}) %collective-permute-start.5) | collective-permute-done | bytes 135200 | tf_op jit(solution)/shard_map/ppermute | solution.py:550
  40.5 0.1 collective-permute-start.6
  40.5 1.3 %collective-permute-done.6.rest_1_ = f32[264,128]{1,0:T(8,128)S(1)} collective-permute-done((f32[264,128]{1,0:T(8,128)S(1)}, f32[264,128]{1,0:T(8,128)S(1)}, u32[]{:S(2)}, u32[]{:S(2)}) %collective-permute-start.6) | collective-permute-done | bytes 135200 | tf_op jit(solution)/shard_map/ppermute | solution.py:550
  41.9 2.0 %collective-permute-done.7.rest_4_ = f32[520,256]{1,0:T(8,128)S(1)} collective-permute-done((f32[520,256]{1,0:T(8,128)S(1)}, f32[520,256]{1,0:T(8,128)S(1)}, u32[]{:S(2)}, u32[]{:S(2)}) %collective-permute-start.7) | collective-permute-done | bytes 532512 | tf_op jit(solution)/shard_map/ppermute | solution.py:550
  43.8 0.0 copy-done.2
  43.8 24.1 %field.1 = (f32[64,4,256]{2,1,0:T(4,128)}, f32[64,64,256]{2,1,0:T(8,128)}) custom-call(s32[3]{0:T(128)S(1)} %pad_add_fusion.meta, s32[64,256]{1,0:T(8,128)S(1)} %copy-done.1, f32[264,128]{1,0:T(8,128)S(1)} %merge.7.rest_0_, f32[264,128]{1,0:T(8,128)S(1)} %collective-permute-done.6.rest_1_, f32[1542,256]{1,0:T(8,128)S(1)} %collective-permute-done.3.near.rest_2_, ...), custom_call_target="tpu_custom_call" | custom-call | flops 8589934592 | bytes 16777216 | tf_op jit(solution)/shard_map/field/pallas_call | solution.py:525
  (7 shorter events, 0.1 us)
Async XLA Ops:
  1.4 4.0 %copy-start = (bf16[64,256,256]{2,1,0:T(8,128)(2,1)S(1)}, bf16[64,256,256]{2,1,0:T(8,128)(2,1)}, u32[]{:S(2)}) copy-start(bf16[64,256,256]{2,1,0:T(8,128)(2,1)} %rest_6_.1) | copy-start | bytes 25165828
  1.4 4.0 %copy-start.1 = (s32[64,256]{1,0:T(8,128)S(1)}, s32[64,256]{1,0:T(8,128)}, u32[]{:S(2)}) copy-start(s32[64,256]{1,0:T(8,128)} %seeds.7) | copy-start | bytes 196612
  3.8 24.2 %collective-permute-start.3 = (f32[1542,256]{1,0:T(8,128)S(1)}, f32[1542,256]{1,0:T(8,128)S(1)}, u32[]{:S(2)}, u32[]{:S(2)}) collective-permute-start(f32[1542,256]{1,0:T(8,128)S(1)} %get-tuple-element.14), channel_id=1, source_target_pairs={{0,1},{1,0},{2,3},{3,2},{4,5},{5,4},{6,7},{7,6},{8,9},{9,8},{10,11... | collective-permute-start | bytes 4737032 | tf_op jit(solution)/shard_map/ppermute | solution.py:550
  4.3 23.7 %collective-permute-start.4 = (f32[1542,256]{1,0:T(8,128)S(1)}, f32[1542,256]{1,0:T(8,128)S(1)}, u32[]{:S(2)}, u32[]{:S(2)}) collective-permute-start(f32[1542,256]{1,0:T(8,128)S(1)} %get-tuple-element.15), channel_id=1, source_target_pairs={{1,4},{4,1},{5,8},{8,5},{9,12},{12,9},{3,6},{6,3},{7,10},{10,7},{1... | collective-permute-start | bytes 4737032 | tf_op jit(solution)/shard_map/ppermute | solution.py:550
  15.5 4.9 %collective-permute-start = (f32[264,128]{1,0:T(8,128)S(1)}, f32[264,128]{1,0:T(8,128)S(1)}, u32[]{:S(2)}, u32[]{:S(2)}) collective-permute-start(f32[264,128]{1,0:T(8,128)S(1)} %get-tuple-element.13), channel_id=1, source_target_pairs={{0,1},{1,0},{2,3},{3,2},{4,5},{5,4},{6,7},{7,6},{8,9},{9,8},{10,11... | collective-permute-start | bytes 405512 | tf_op jit(solution)/shard_map/ppermute | solution.py:550
  20.4 5.9 %collective-permute-start.1 = (f32[264,128]{1,0:T(8,128)S(1)}, f32[264,128]{1,0:T(8,128)S(1)}, u32[]{:S(2)}, u32[]{:S(2)}) collective-permute-start(f32[264,128]{1,0:T(8,128)S(1)} %merge.4.a), channel_id=1, source_target_pairs={{0,2},{2,0},{1,3},{3,1},{4,6},{6,4},{5,7},{7,5},{8,10},{10,8},{9,1... | collective-permute-start | bytes 405512 | tf_op jit(solution)/shard_map/ppermute | solution.py:550
  26.4 17.5 %copy-start.2 = (bf16[2,768,384]{2,1,0:T(8,128)(2,1)S(1)}, bf16[2,768,384]{2,1,0:T(8,128)(2,1)}, u32[]{:S(2)}) copy-start(bf16[2,768,384]{2,1,0:T(8,128)(2,1)} %constant.21.clone.rest_5_) | copy-start | bytes 3538948
  26.4 5.1 %collective-permute-start.2 = (f32[264,128]{1,0:T(8,128)S(1)}, f32[264,128]{1,0:T(8,128)S(1)}, u32[]{:S(2)}, u32[]{:S(2)}) collective-permute-start(f32[264,128]{1,0:T(8,128)S(1)} %merge.5.a), channel_id=1, source_target_pairs={{0,4},{4,0},{8,12},{12,8},{1,5},{5,1},{9,13},{13,9},{2,6},{6,2},{1... | collective-permute-start | bytes 405512 | tf_op jit(solution)/shard_map/ppermute | solution.py:550
  31.5 12.4 %collective-permute-start.7 = (f32[520,256]{1,0:T(8,128)S(1)}, f32[520,256]{1,0:T(8,128)S(1)}, u32[]{:S(2)}, u32[]{:S(2)}) collective-permute-start(f32[520,256]{1,0:T(8,128)S(1)} %side.1), channel_id=1, source_target_pairs={{0,2},{2,0},{1,3},{3,1},{4,6},{6,4},{5,7},{7,5},{8,10},{10,8},{9,1... | collective-permute-start | bytes 1597448 | tf_op jit(solution)/shard_map/ppermute | solution.py:550
  33.0 7.4 %collective-permute-start.5 = (f32[264,128]{1,0:T(8,128)S(1)}, f32[264,128]{1,0:T(8,128)S(1)}, u32[]{:S(2)}, u32[]{:S(2)}) collective-permute-start(f32[264,128]{1,0:T(8,128)S(1)} %merge.6.a), channel_id=1, source_target_pairs={{0,8},{8,0},{4,12},{12,4},{1,9},{9,1},{5,13},{13,5},{2,10},{10,2},... | collective-permute-start | bytes 405512 | tf_op jit(solution)/shard_map/ppermute | solution.py:550
  40.5 1.4 %collective-permute-start.6 = (f32[264,128]{1,0:T(8,128)S(1)}, f32[264,128]{1,0:T(8,128)S(1)}, u32[]{:S(2)}, u32[]{:S(2)}) collective-permute-start(f32[264,128]{1,0:T(8,128)S(1)} %merge.7.rest_0_), channel_id=1, source_target_pairs={{0,1},{1,0},{2,3},{3,2},{4,5},{5,4},{6,7},{7,6},{8,9},{9,8},{10,11... | collective-permute-start | bytes 405512 | tf_op jit(solution)/shard_map/ppermute | solution.py:550

commit v4 on v3

--- a/solution.py
+++ b/solution.py
@@ -424,7 +424,7 @@
                     value = jnp.where(lane < EDGE + SIDE, value, more)
                 ref[row, :, cols:] = value
 
-    rows = 16
+    rows = 32
 
     @pl.loop(0, height // rows)
     def _(i):

time: 68.3 us -> 68 us (level)
  no operation moved by 1% of the time
where the time goes in v4:
time: 68 us; the launch traced here: 67.8 us
  Pallas kernels  37.5 us (55%)
  waiting for transfers between devices  15.9 us (23%)
  starting transfers between devices  12.6 us (19%)
  between operations  1.53 us (2%)
    pallas_call x1, Pallas kernels, field(): pl.pallas_call(functools.partial(field_kernel, sides=len(strips)), out_sh...  23.8 us
    ppermute x8, waiting for transfers between devices, swap(): lax.ppermute(x, axes, [p for a, b in pairs for p in ((a, b), (b, a))])  15.9 us
    ppermute x8, starting transfers between devices, swap(): lax.ppermute(x, axes, [p for a, b in pairs for p in ((a, b), (b, a))])  12.6 us
    pallas_call x1, Pallas kernels, pool(): pl.pallas_call(functools.partial(pool_kernel, rows=rows), out_shape=(piec...  10.2 us
    pallas_call x1, Pallas kernels, ends(): pl.pallas_call(ends_kernel, out_shape=(message, message, jax.ShapeDtypeSt...  2.45 us
  transfers between devices with their start and end apart: 8, of which 6 were waited for; matrix products, arithmetic and copies ran while one was open for 0% of the time, Pallas kernels for 17%

profile of v4, /device:TPU:0, one launch (start us, length us, event | category | flops | bytes accessed | tf_op | source)
XLA Modules:
  0.0 67.8 jit_solution(7807442454543479635)
XLA Ops:
  1.3 0.1 pad_add_fusion.meta
  1.4 2.5 %ends.1 = (f32[1542,256]{1,0:T(8,128)S(1)}, f32[1542,256]{1,0:T(8,128)S(1)}, bf16[256,256]{1,0:T(8,128)(2,1)S(1)}) custom-call(s32[3]{0:T(128)S(1)} %pad_add_fusion.meta, s32[64,256]{1,0:T(8,128)} %seeds.7, bf16[64,256,256]{2,1,0:T(8,128)(2,1)} %rest_6_.1, bf16[64,4,256]{2,1,0:T(4,128)(2,1)} %given.1), custom_call_target="tpu_custom_call" | custom-call | bytes 4194304 | tf_op jit(solution)/shard_map/ends/pallas_call | solution.py:119
  3.8 0.5 collective-permute-start.3
  4.3 0.8 %collective-permute-start.4 = (f32[1542,256]{1,0:T(8,128)S(1)}, f32[1542,256]{1,0:T(8,128)S(1)}, u32[]{:S(2)}, u32[]{:S(2)}) collective-permute-start(f32[1542,256]{1,0:T(8,128)S(1)} %get-tuple-element.15), channel_id=1, source_target_pairs={{1,4},{4,1},{5,8},{8,5},{9,12},{12,9},{3,6},{6,3},{7,10},{10,7},{1... | collective-permute-start | bytes 4737032 | tf_op jit(solution)/shard_map/ppermute | solution.py:550
  5.1 0.2 copy-done
  5.3 10.2 %pool.1 = (f32[264,128]{1,0:T(8,128)S(1)}, f32[264,128]{1,0:T(8,128)S(1)}) custom-call(s32[3]{0:T(128)S(1)} %pad_add_fusion.meta, s32[64,256]{1,0:T(8,128)S(1)} %copy-done.1, bf16[64,256,256]{2,1,0:T(8,128)(2,1)S(1)} %copy-done, bf16[256,256]{1,0:T(8,128)(2,1)S(1)} %get-tuple-element.11.protos), custom_call_target="tpu_custom_call" | custom-call | flops 4294967296 | bytes 8388608 | tf_op jit(solution)/shard_map/pool/pallas_call | solution.py:311
  15.5 3.9 %collective-permute-start = (f32[264,128]{1,0:T(8,128)S(1)}, f32[264,128]{1,0:T(8,128)S(1)}, u32[]{:S(2)}, u32[]{:S(2)}) collective-permute-start(f32[264,128]{1,0:T(8,128)S(1)} %get-tuple-element.13), channel_id=1, source_target_pairs={{0,1},{1,0},{2,3},{3,2},{4,5},{5,4},{6,7},{7,6},{8,9},{9,8},{10,11... | collective-permute-start | bytes 405512 | tf_op jit(solution)/shard_map/ppermute | solution.py:550
  19.4 1.0 %collective-permute-done.b = f32[264,128]{1,0:T(8,128)S(1)} collective-permute-done((f32[264,128]{1,0:T(8,128)S(1)}, f32[264,128]{1,0:T(8,128)S(1)}, u32[]{:S(2)}, u32[]{:S(2)}) %collective-permute-start) | collective-permute-done | bytes 135200 | tf_op jit(solution)/shard_map/ppermute | solution.py:550
  20.4 1.6 %collective-permute-start.1 = (f32[264,128]{1,0:T(8,128)S(1)}, f32[264,128]{1,0:T(8,128)S(1)}, u32[]{:S(2)}, u32[]{:S(2)}) collective-permute-start(f32[264,128]{1,0:T(8,128)S(1)} %merge.4.a), channel_id=1, source_target_pairs={{0,2},{2,0},{1,3},{3,1},{4,6},{6,4},{5,7},{7,5},{8,10},{10,8},{9,1... | collective-permute-start | bytes 405512 | tf_op jit(solution)/shard_map/ppermute | solution.py:550
  22.0 4.3 %collective-permute-done.1.b = f32[264,128]{1,0:T(8,128)S(1)} collective-permute-done((f32[264,128]{1,0:T(8,128)S(1)}, f32[264,128]{1,0:T(8,128)S(1)}, u32[]{:S(2)}, u32[]{:S(2)}) %collective-permute-start.1) | collective-permute-done | bytes 135200 | tf_op jit(solution)/shard_map/ppermute | solution.py:550
  26.4 0.0 copy-start.2
  26.4 1.6 %collective-permute-start.2 = (f32[264,128]{1,0:T(8,128)S(1)}, f32[264,128]{1,0:T(8,128)S(1)}, u32[]{:S(2)}, u32[]{:S(2)}) collective-permute-start(f32[264,128]{1,0:T(8,128)S(1)} %merge.5.a), channel_id=1, source_target_pairs={{0,4},{4,0},{8,12},{12,8},{1,5},{5,1},{9,13},{13,9},{2,6},{6,2},{1... | collective-permute-start | bytes 405512 | tf_op jit(solution)/shard_map/ppermute | solution.py:550
  28.0 0.0 collective-permute-done.3.near.rest_2_
  28.0 0.0 collective-permute-done.4.far.rest_3_
  28.0 1.0 %side.1 = f32[520,256]{1,0:T(8,128)S(1)} custom-call(s32[3]{0:T(128)S(1)} %pad_add_fusion.meta, s32[64,256]{1,0:T(8,128)S(1)} %copy-done.1, f32[1542,256]{1,0:T(8,128)S(1)} %collective-permute-done.3.near.rest_2_, f32[1542,256]{1,0:T(8,128)S(1)} %collective-permute-done.4.far.rest_3_, bf16[64,256,256]{2,1,0:T(8,128)(2,1)S(1)} %copy-done), custom_call_target="tpu_custom_call" | custom-call | bytes 2097152 | tf_op jit(solution)/shard_map/side/pallas_call | solution.py:202
  29.0 2.5 %collective-permute-done.2.b = f32[264,128]{1,0:T(8,128)S(1)} collective-permute-done((f32[264,128]{1,0:T(8,128)S(1)}, f32[264,128]{1,0:T(8,128)S(1)}, u32[]{:S(2)}, u32[]{:S(2)}) %collective-permute-start.2) | collective-permute-done | bytes 135200 | tf_op jit(solution)/shard_map/ppermute | solution.py:550
  31.5 1.5 %collective-permute-start.7 = (f32[520,256]{1,0:T(8,128)S(1)}, f32[520,256]{1,0:T(8,128)S(1)}, u32[]{:S(2)}, u32[]{:S(2)}) collective-permute-start(f32[520,256]{1,0:T(8,128)S(1)} %side.1), channel_id=1, source_target_pairs={{0,2},{2,0},{1,3},{3,1},{4,6},{6,4},{5,7},{7,5},{8,10},{10,8},{9,1... | collective-permute-start | bytes 1597448 | tf_op jit(solution)/shard_map/ppermute | solution.py:550
  33.0 2.7 %collective-permute-start.5 = (f32[264,128]{1,0:T(8,128)S(1)}, f32[264,128]{1,0:T(8,128)S(1)}, u32[]{:S(2)}, u32[]{:S(2)}) collective-permute-start(f32[264,128]{1,0:T(8,128)S(1)} %merge.6.a), channel_id=1, source_target_pairs={{0,8},{8,0},{4,12},{12,4},{1,9},{9,1},{5,13},{13,5},{2,10},{10,2},... | collective-permute-start | bytes 405512 | tf_op jit(solution)/shard_map/ppermute | solution.py:550
  35.6 4.8 %collective-permute-done.5.b = f32[264,128]{1,0:T(8,128)S(1)} collective-permute-done((f32[264,128]{1,0:T(8,128)S(1)}, f32[264,128]{1,0:T(8,128)S(1)}, u32[]{:S(2)}, u32[]{:S(2)}) %collective-permute-start.5) | collective-permute-done | bytes 135200 | tf_op jit(solution)/shard_map/ppermute | solution.py:550
  40.5 0.1 collective-permute-start.6
  40.5 1.3 %collective-permute-done.6.rest_1_ = f32[264,128]{1,0:T(8,128)S(1)} collective-permute-done((f32[264,128]{1,0:T(8,128)S(1)}, f32[264,128]{1,0:T(8,128)S(1)}, u32[]{:S(2)}, u32[]{:S(2)}) %collective-permute-start.6) | collective-permute-done | bytes 135200 | tf_op jit(solution)/shard_map/ppermute | solution.py:550
  41.9 2.0 %collective-permute-done.7.rest_4_ = f32[520,256]{1,0:T(8,128)S(1)} collective-permute-done((f32[520,256]{1,0:T(8,128)S(1)}, f32[520,256]{1,0:T(8,128)S(1)}, u32[]{:S(2)}, u32[]{:S(2)}) %collective-permute-start.7) | collective-permute-done | bytes 532512 | tf_op jit(solution)/shard_map/ppermute | solution.py:550
  43.8 0.0 copy-done.2
  43.8 23.8 %field.1 = (f32[64,4,256]{2,1,0:T(4,128)}, f32[64,64,256]{2,1,0:T(8,128)}) custom-call(s32[3]{0:T(128)S(1)} %pad_add_fusion.meta, s32[64,256]{1,0:T(8,128)S(1)} %copy-done.1, f32[264,128]{1,0:T(8,128)S(1)} %merge.7.rest_0_, f32[264,128]{1,0:T(8,128)S(1)} %collective-permute-done.6.rest_1_, f32[1542,256]{1,0:T(8,128)S(1)} %collective-permute-done.3.near.rest_2_, ...), custom_call_target="tpu_custom_call" | custom-call | flops 8589934592 | bytes 16777216 | tf_op jit(solution)/shard_map/field/pallas_call | solution.py:525
  (7 shorter events, 0.1 us)
Async XLA Ops:
  1.4 4.0 %copy-start = (bf16[64,256,256]{2,1,0:T(8,128)(2,1)S(1)}, bf16[64,256,256]{2,1,0:T(8,128)(2,1)}, u32[]{:S(2)}) copy-start(bf16[64,256,256]{2,1,0:T(8,128)(2,1)} %rest_6_.1) | copy-start | bytes 25165828
  1.4 4.0 %copy-start.1 = (s32[64,256]{1,0:T(8,128)S(1)}, s32[64,256]{1,0:T(8,128)}, u32[]{:S(2)}) copy-start(s32[64,256]{1,0:T(8,128)} %seeds.7) | copy-start | bytes 196612
  3.8 24.2 %collective-permute-start.3 = (f32[1542,256]{1,0:T(8,128)S(1)}, f32[1542,256]{1,0:T(8,128)S(1)}, u32[]{:S(2)}, u32[]{:S(2)}) collective-permute-start(f32[1542,256]{1,0:T(8,128)S(1)} %get-tuple-element.14), channel_id=1, source_target_pairs={{0,1},{1,0},{2,3},{3,2},{4,5},{5,4},{6,7},{7,6},{8,9},{9,8},{10,11... | collective-permute-start | bytes 4737032 | tf_op jit(solution)/shard_map/ppermute | solution.py:550
  4.3 23.7 %collective-permute-start.4 = (f32[1542,256]{1,0:T(8,128)S(1)}, f32[1542,256]{1,0:T(8,128)S(1)}, u32[]{:S(2)}, u32[]{:S(2)}) collective-permute-start(f32[1542,256]{1,0:T(8,128)S(1)} %get-tuple-element.15), channel_id=1, source_target_pairs={{1,4},{4,1},{5,8},{8,5},{9,12},{12,9},{3,6},{6,3},{7,10},{10,7},{1... | collective-permute-start | bytes 4737032 | tf_op jit(solution)/shard_map/ppermute | solution.py:550
  15.5 4.9 %collective-permute-start = (f32[264,128]{1,0:T(8,128)S(1)}, f32[264,128]{1,0:T(8,128)S(1)}, u32[]{:S(2)}, u32[]{:S(2)}) collective-permute-start(f32[264,128]{1,0:T(8,128)S(1)} %get-tuple-element.13), channel_id=1, source_target_pairs={{0,1},{1,0},{2,3},{3,2},{4,5},{5,4},{6,7},{7,6},{8,9},{9,8},{10,11... | collective-permute-start | bytes 405512 | tf_op jit(solution)/shard_map/ppermute | solution.py:550
  20.4 5.9 %collective-permute-start.1 = (f32[264,128]{1,0:T(8,128)S(1)}, f32[264,128]{1,0:T(8,128)S(1)}, u32[]{:S(2)}, u32[]{:S(2)}) collective-permute-start(f32[264,128]{1,0:T(8,128)S(1)} %merge.4.a), channel_id=1, source_target_pairs={{0,2},{2,0},{1,3},{3,1},{4,6},{6,4},{5,7},{7,5},{8,10},{10,8},{9,1... | collective-permute-start | bytes 405512 | tf_op jit(solution)/shard_map/ppermute | solution.py:550
  26.4 17.5 %copy-start.2 = (bf16[2,768,384]{2,1,0:T(8,128)(2,1)S(1)}, bf16[2,768,384]{2,1,0:T(8,128)(2,1)}, u32[]{:S(2)}) copy-start(bf16[2,768,384]{2,1,0:T(8,128)(2,1)} %constant.21.clone.rest_5_) | copy-start | bytes 3538948
  26.4 5.1 %collective-permute-start.2 = (f32[264,128]{1,0:T(8,128)S(1)}, f32[264,128]{1,0:T(8,128)S(1)}, u32[]{:S(2)}, u32[]{:S(2)}) collective-permute-start(f32[264,128]{1,0:T(8,128)S(1)} %merge.5.a), channel_id=1, source_target_pairs={{0,4},{4,0},{8,12},{12,8},{1,5},{5,1},{9,13},{13,9},{2,6},{6,2},{1... | collective-permute-start | bytes 405512 | tf_op jit(solution)/shard_map/ppermute | solution.py:550
  31.5 12.4 %collective-permute-start.7 = (f32[520,256]{1,0:T(8,128)S(1)}, f32[520,256]{1,0:T(8,128)S(1)}, u32[]{:S(2)}, u32[]{:S(2)}) collective-permute-start(f32[520,256]{1,0:T(8,128)S(1)} %side.1), channel_id=1, source_target_pairs={{0,2},{2,0},{1,3},{3,1},{4,6},{6,4},{5,7},{7,5},{8,10},{10,8},{9,1... | collective-permute-start | bytes 1597448 | tf_op jit(solution)/shard_map/ppermute | solution.py:550
  33.0 7.4 %collective-permute-start.5 = (f32[264,128]{1,0:T(8,128)S(1)}, f32[264,128]{1,0:T(8,128)S(1)}, u32[]{:S(2)}, u32[]{:S(2)}) collective-permute-start(f32[264,128]{1,0:T(8,128)S(1)} %merge.6.a), channel_id=1, source_target_pairs={{0,8},{8,0},{4,12},{12,4},{1,9},{9,1},{5,13},{13,5},{2,10},{10,2},... | collective-permute-start | bytes 405512 | tf_op jit(solution)/shard_map/ppermute | solution.py:550
  40.5 1.4 %collective-permute-start.6 = (f32[264,128]{1,0:T(8,128)S(1)}, f32[264,128]{1,0:T(8,128)S(1)}, u32[]{:S(2)}, u32[]{:S(2)}) collective-permute-start(f32[264,128]{1,0:T(8,128)S(1)} %merge.7.rest_0_), channel_id=1, source_target_pairs={{0,1},{1,0},{2,3},{3,2},{4,5},{5,4},{6,7},{7,6},{8,9},{9,8},{10,11... | collective-permute-start | bytes 405512 | tf_op jit(solution)/shard_map/ppermute | solution.py:550
